TPU v7x, 128 devices: a whole 4x4x4 slice. The times are simulated.
128 devices in a mesh: image: 4 (over y), token: 32 (over z, x, core).
Axes of the slice: x: 4, y: 4, z: 4, core: 2. Of those that a mesh axis runs over, the one named last changes fastest.
Arguments:
- hidden: bfloat16 [2, 4, 4096, 3072], P(None, 'image', 'token'), may hold values from -6 to 6
- key_cache: bfloat16 [2, 4, 4096, 1536], P(None, 'image', 'token')
- value_cache: bfloat16 [2, 4, 4096, 1536], P(None, 'image', 'token'), may hold values from -6 to 6
- cached_out: bfloat16 [4, 4096, 1536], P('image', 'token'), may hold values from -6 to 6
- w_query: bfloat16 [3072, 1536], P('image'), may hold values from -0.109375 to 0.109375
- guide: float32 [4], P('image'), may hold values from 1.5 to 4
- masked_tiles: int32 [4, 8], P('image'), may hold values from 0 to 31, as said below
- mask_count: int32 [4], P('image'), may hold values from 4 to 8, as said below
Outputs:
- edited: bfloat16 [4, 4096, 1536], P('image', 'token')
Inputs may be any that keep to these rules, and one draw needn't show every extreme that they name: `masked_tiles`: in each image the first mask_count entries are distinct tiles; later entries are tiles too. `mask_count`: some image of every draw has exactly 8 masked tiles.
All inputs are finite; a program needn't handle non-finite values.
Results may differ from a plain program's by a relative error of at most 0.011.
The roundings to bfloat16 on the way count: a program that leaves them out, or rounds other values in their place, can miss the bound.
Values may be sent and summed in bfloat16 or wider, within the bound.
A program may use at most 128 MiB of HBM per device.

v0:
```python
import math

import jax
import jax.numpy as jnp
from jax import lax
from jax.sharding import PartitionSpec as P

HD = 128
TILE = 128


def spread(array, axis, root):
    mine = lax.axis_index(axis) == root
    return lax.psum(jnp.where(mine, array, jnp.zeros_like(array)), axis)


def body(hidden, key_cache, value_cache, cached_out, w_query, guide, masked_tiles, mask_count):
    position = lax.axis_index("token")
    images = hidden.shape[1]
    tok_dev = hidden.shape[2]
    model_width = hidden.shape[3]
    inner_width = key_cache.shape[3]
    head_count = inner_width // HD
    per_dev = tok_dev // TILE
    slot_most = masked_tiles.shape[1]
    slot_total = images * slot_most
    scale_for_scores = 1.0 / math.sqrt(HD)
    flattened = hidden.reshape(2 * images * tok_dev, model_width)
    query_sum = jnp.dot(
        flattened,
        lax.all_gather(w_query, "image", axis=0, tiled=True),
        preferred_element_type=jnp.float32,
    )
    own_query = query_sum.astype(jnp.bfloat16).reshape(2, images, per_dev, TILE, inner_width)
    slot_tile = masked_tiles.reshape(slot_total)
    slot_image = jnp.arange(slot_total, dtype=jnp.int32) // slot_most
    slot_owner = slot_tile // per_dev
    slot_local = slot_tile % per_dev

    def send_one(slot_index, gathered):
        picked = own_query[:, slot_image[slot_index], slot_local[slot_index]]
        arrived = spread(picked, "token", slot_owner[slot_index])
        return lax.dynamic_update_index_in_dim(gathered, arrived, slot_index, 1)

    queries = lax.fori_loop(
        0, slot_total, send_one, jnp.zeros((2, slot_total, TILE, inner_width), jnp.bfloat16)
    )
    query_heads = queries.reshape(2, images, slot_most, TILE, head_count, HD)
    key_block = key_cache.reshape(2, images, tok_dev, head_count, HD)
    value_block = value_cache.reshape(2, images, tok_dev, head_count, HD)
    logit_scores = (
        jnp.einsum(
            "bimrhd,bikhd->bimhrk", query_heads, key_block, preferred_element_type=jnp.float32
        )
        * scale_for_scores
    )
    local_max = jnp.max(logit_scores, axis=-1)
    row_max = lax.pmax(local_max.astype(jnp.bfloat16), "token").astype(local_max.dtype)
    exp_scores = jnp.exp(logit_scores - row_max[..., None])
    row_total = lax.psum(jnp.sum(exp_scores, axis=-1).astype(jnp.bfloat16), "token").astype(
        jnp.float32
    )
    softmax_weights = (exp_scores / row_total[..., None]).astype(jnp.bfloat16)
    attended = jnp.einsum(
        "bimhrk,bikhd->bimrhd", softmax_weights, value_block, preferred_element_type=jnp.float32
    )
    attended = attended.reshape(2, images, slot_most, TILE, inner_width)
    guide_scale = guide[:, None, None, None]
    guided_part = attended[1] + guide_scale * (attended[0] - attended[1])
    guided_part = guided_part.reshape(slot_total * TILE, inner_width)
    summed_rows = lax.psum(guided_part, "token")
    result = summed_rows.astype(jnp.bfloat16)
    result = result.reshape(images, slot_most, TILE, inner_width)
    tile_ids = position * per_dev + jnp.arange(per_dev, dtype=jnp.int32)
    in_use = jnp.arange(slot_most, dtype=jnp.int32)[None, :] < mask_count[:, None]
    matched = (masked_tiles[:, None, :] == tile_ids[None, :, None]) & in_use[:, None, :]
    chosen = jnp.einsum(
        "iuj,ijrc->iurc", matched.astype(jnp.bfloat16), result, preferred_element_type=jnp.float32
    )
    pasted_mask = jnp.any(matched, axis=-1)[:, :, None, None]
    previous = cached_out.reshape(images, per_dev, TILE, inner_width)
    edited = jnp.where(pasted_mask, chosen.astype(jnp.bfloat16), previous)
    return edited.reshape(images, tok_dev, inner_width)


def solution(mesh):
    return jax.shard_map(
        body,
        mesh=mesh,
        in_specs=(
            P(None, "image", "token", None),
            P(None, "image", "token", None),
            P(None, "image", "token", None),
            P("image", "token", None),
            P("image", None),
            P("image"),
            P("image", None),
            P("image"),
        ),
        out_specs=P("image", "token", None),
        check_vma=False,
    )
```

profile of v0, /device:TPU:1, one launch (start us, length us, event | category | flops | bytes accessed | tf_op | source)
XLA Modules:
  0.0 1469.7 jit_solution(158046742337327295)
XLA Ops:
  7.3 1.5 copy.14
  8.8 2.3 copy.17
  13.8 90.2 %all-gather.2.cloned.1.call-done = bf16[3072,1536]{1,0:T(8,128)(2,1)} async-done(((bf16[768,1536]{1,0:T(8,128)(2,1)}), bf16[3072,1536]{1,0:T(8,128)(2,1)}) %all-gather.2.cloned.1.call-update) | async-done | bytes 9437200 | tf_op jit(solution)/shard_map/all_gather | solution.py:31
  104.0 6.3 convolution_convert_fusion
  110.3 885.3 %while.13 = (s32[]{:T(128)}, bf16[2,8,128,1536]{2,3,1,0:T(8,128)(2,1)}, s32[8]{0:T(128)S(1)}, bf16[2,1,1,128,1536]{4,3,0,2,1:T(8,128)(2,1)S(1)}, s32[]{:T(128)}, /*index=5*/u32[]{:T(128)}) while((s32[]{:T(128)}, bf16[2,8,128,1536]{2,3,1,0:T(8,128)(2,1)}, s32[8]{0:T(128)S(1)}, bf16[2,1,1,128,1536]{4,3,0,2,1:T(8,128)(2,1)S(1)}, s32[]{:T(128)}, ...), condition=%wide.region_3.4_spmd, body=%wide.region_1.3_spmd.sunk | while | flops 786437 | bytes 9437347 | solution.py:45
  112.6 107.4 %all-reduce.3.cloned.1.call-done = bf16[2,1,128,1536]{3,2,1,0:T(8,128)(2,1)} async-done(((bf16[2,1,128,1536]{3,2,1,0:T(8,128)(2,1)}), bf16[2,1,128,1536]{3,2,1,0:T(8,128)(2,1)}) %all-reduce.3.cloned.1.call-update) | async-done | bytes 786448 | tf_op jit(solution)/shard_map/while/body/eval_jaxpr/psum | solution.py:14
  220.0 1.5 copy.44
  224.7 105.9 %all-reduce.3.cloned.1.call-done = bf16[2,1,128,1536]{3,2,1,0:T(8,128)(2,1)} async-done(((bf16[2,1,128,1536]{3,2,1,0:T(8,128)(2,1)}), bf16[2,1,128,1536]{3,2,1,0:T(8,128)(2,1)}) %all-reduce.3.cloned.1.call-update) | async-done | bytes 786448 | tf_op jit(solution)/shard_map/while/body/eval_jaxpr/psum | solution.py:14
  330.6 1.5 copy.44
  335.3 105.6 %all-reduce.3.cloned.1.call-done = bf16[2,1,128,1536]{3,2,1,0:T(8,128)(2,1)} async-done(((bf16[2,1,128,1536]{3,2,1,0:T(8,128)(2,1)}), bf16[2,1,128,1536]{3,2,1,0:T(8,128)(2,1)}) %all-reduce.3.cloned.1.call-update) | async-done | bytes 786448 | tf_op jit(solution)/shard_map/while/body/eval_jaxpr/psum | solution.py:14
  440.9 1.5 copy.44
  445.6 105.6 %all-reduce.3.cloned.1.call-done = bf16[2,1,128,1536]{3,2,1,0:T(8,128)(2,1)} async-done(((bf16[2,1,128,1536]{3,2,1,0:T(8,128)(2,1)}), bf16[2,1,128,1536]{3,2,1,0:T(8,128)(2,1)}) %all-reduce.3.cloned.1.call-update) | async-done | bytes 786448 | tf_op jit(solution)/shard_map/while/body/eval_jaxpr/psum | solution.py:14
  551.2 1.5 copy.44
  555.8 105.6 %all-reduce.3.cloned.1.call-done = bf16[2,1,128,1536]{3,2,1,0:T(8,128)(2,1)} async-done(((bf16[2,1,128,1536]{3,2,1,0:T(8,128)(2,1)}), bf16[2,1,128,1536]{3,2,1,0:T(8,128)(2,1)}) %all-reduce.3.cloned.1.call-update) | async-done | bytes 786448 | tf_op jit(solution)/shard_map/while/body/eval_jaxpr/psum | solution.py:14
  661.4 1.5 copy.44
  666.1 105.9 %all-reduce.3.cloned.1.call-done = bf16[2,1,128,1536]{3,2,1,0:T(8,128)(2,1)} async-done(((bf16[2,1,128,1536]{3,2,1,0:T(8,128)(2,1)}), bf16[2,1,128,1536]{3,2,1,0:T(8,128)(2,1)}) %all-reduce.3.cloned.1.call-update) | async-done | bytes 786448 | tf_op jit(solution)/shard_map/while/body/eval_jaxpr/psum | solution.py:14
  772.0 1.5 copy.44
  776.6 105.9 %all-reduce.3.cloned.1.call-done = bf16[2,1,128,1536]{3,2,1,0:T(8,128)(2,1)} async-done(((bf16[2,1,128,1536]{3,2,1,0:T(8,128)(2,1)}), bf16[2,1,128,1536]{3,2,1,0:T(8,128)(2,1)}) %all-reduce.3.cloned.1.call-update) | async-done | bytes 786448 | tf_op jit(solution)/shard_map/while/body/eval_jaxpr/psum | solution.py:14
  882.5 1.5 copy.44
  887.2 105.9 %all-reduce.3.cloned.1.call-done = bf16[2,1,128,1536]{3,2,1,0:T(8,128)(2,1)} async-done(((bf16[2,1,128,1536]{3,2,1,0:T(8,128)(2,1)}), bf16[2,1,128,1536]{3,2,1,0:T(8,128)(2,1)}) %all-reduce.3.cloned.1.call-update) | async-done | bytes 786448 | tf_op jit(solution)/shard_map/while/body/eval_jaxpr/psum | solution.py:14
  993.1 1.5 copy.44
  995.6 9.2 bitcast_reduce_fusion
  1004.8 122.2 %pmax.7 = bf16[2,8,12,128]{3,1,2,0:T(8,128)(2,1)S(1)} all-reduce(bf16[2,8,12,128]{3,1,2,0:T(8,128)(2,1)S(1)} %get-tuple-element.117), channel_id=1, replica_groups=mesh['image'=4,'token'=32] {'token'}, use_global_device_ids=true, to_apply=%region_5.6 | all-reduce | flops 24576 | bytes 98304 | tf_op jit(solution)/shard_map/pmax | solution.py:58
  1127.0 8.7 fusion.1
  1135.7 124.0 %psum.25 = bf16[2,8,12,128]{3,1,2,0:T(8,128)(2,1)S(1)} all-reduce(bf16[2,8,12,128]{3,1,2,0:T(8,128)(2,1)S(1)} %fusion.1), channel_id=1, replica_groups=mesh['image'=4,'token'=32] {'token'}, use_global_device_ids=true, to_apply=%region_7.8 | all-reduce | flops 24576 | bytes 98304 | tf_op jit(solution)/shard_map/psum | solution.py:60
  1259.8 12.0 fusion.10
  1271.8 11.3 fusion.19
  1283.1 6.6 copy.20
  1289.7 6.6 copy.21
  1296.3 10.4 fusion.3
  1306.7 150.7 %all-reduce.4 = bf16[1024,1536]{0,1:T(8,128)(2,1)} all-reduce(f32[1024,1536]{0,1:T(8,128)} %fusion.3), channel_id=1, replica_groups=mesh['image'=4,'token'=32] {'token'}, use_global_device_ids=true, to_apply=%region_8.9 | all-reduce | flops 1572864 | bytes 9437184 | tf_op jit(solution)/shard_map/psum | solution.py:71
  1457.4 2.8 copy.36
  (59 shorter events, 25.2 us)
Async XLA Ops:
  6.5 97.4 %copy-start = (bf16[2,1,128,3072]{3,2,1,0:T(8,128)(2,1)S(1)}, bf16[2,1,128,3072]{3,2,1,0:T(8,128)(2,1)}, u32[]{:S(2)}) copy-start(bf16[2,1,128,3072]{3,2,1,0:T(8,128)(2,1)} %param.10) | copy-start | bytes 4718596
  6.5 97.4 %all-gather.2.cloned.1.call-start = ((), (), s32[]{:S(2)}) async-start(), calls=%async_computation | async-start | bytes 11796480 | tf_op jit(solution)/shard_map/all_gather | solution.py:31
  104.0 6.3 copy-start.4
  110.3 109.7 %all-reduce.3.cloned.1.call-start = ((), (), s32[]{:S(2)}) async-start(), calls=%async_computation.1 | async-start | bytes 1572864 | tf_op jit(solution)/shard_map/while/body/eval_jaxpr/psum | solution.py:14
  222.5 108.1 %all-reduce.3.cloned.1.call-start = ((), (), s32[]{:S(2)}) async-start(), calls=%async_computation.1 | async-start | bytes 1572864 | tf_op jit(solution)/shard_map/while/body/eval_jaxpr/psum | solution.py:14
  333.1 107.8 %all-reduce.3.cloned.1.call-start = ((), (), s32[]{:S(2)}) async-start(), calls=%async_computation.1 | async-start | bytes 1572864 | tf_op jit(solution)/shard_map/while/body/eval_jaxpr/psum | solution.py:14
  443.4 107.8 %all-reduce.3.cloned.1.call-start = ((), (), s32[]{:S(2)}) async-start(), calls=%async_computation.1 | async-start | bytes 1572864 | tf_op jit(solution)/shard_map/while/body/eval_jaxpr/psum | solution.py:14
  553.6 107.8 %all-reduce.3.cloned.1.call-start = ((), (), s32[]{:S(2)}) async-start(), calls=%async_computation.1 | async-start | bytes 1572864 | tf_op jit(solution)/shard_map/while/body/eval_jaxpr/psum | solution.py:14
  663.8 108.1 %all-reduce.3.cloned.1.call-start = ((), (), s32[]{:S(2)}) async-start(), calls=%async_computation.1 | async-start | bytes 1572864 | tf_op jit(solution)/shard_map/while/body/eval_jaxpr/psum | solution.py:14
  774.4 108.1 %all-reduce.3.cloned.1.call-start = ((), (), s32[]{:S(2)}) async-start(), calls=%async_computation.1 | async-start | bytes 1572864 | tf_op jit(solution)/shard_map/while/body/eval_jaxpr/psum | solution.py:14
  885.0 108.1 %all-reduce.3.cloned.1.call-start = ((), (), s32[]{:S(2)}) async-start(), calls=%async_computation.1 | async-start | bytes 1572864 | tf_op jit(solution)/shard_map/while/body/eval_jaxpr/psum | solution.py:14
  1127.0 132.7 %copy-start.2 = (bf16[2,1,128,1536]{2,3,0,1:T(8,128)(2,1)S(1)}, bf16[2,1,128,1536]{2,3,0,1:T(8,128)(2,1)}, u32[]{:S(2)}) copy-start(bf16[2,1,128,1536]{2,3,0,1:T(8,128)(2,1)} %copy.17) | copy-start | bytes 2359300
  1457.4 4.4 copy-start.3
  1457.4 5.8 copy-start.1
Sparse Core Ops, SparseCore 0:
  9.0 94.9 all-gather.1
  114.4 105.6 all-reduce.2
  226.5 104.0 all-reduce.2
  336.8 104.0 all-reduce.2
  447.1 104.0 all-reduce.2
  557.3 104.0 all-reduce.2
  667.9 104.0 all-reduce.2
  778.5 104.0 all-reduce.2
  889.1 104.0 all-reduce.2
where the time goes:
time: 1480 us; the launch traced here: 1470 us
  waiting for transfers between devices  939 us (63%)
  blocking collectives  397 us (27%)
  local copies, waits for them, and re-layouts  56 us (4%)
  other arithmetic  29.6 us (2%)
  matrix products  28.5 us (2%)
    psum x8, waiting for transfers between devices, spread(): return lax.psum(jnp.where(mine, array, jnp.zeros_like(array)), axis)  848 us
    psum x1, blocking collectives, body(): summed_rows = lax.psum(guided_part, 'token')  151 us
    psum x1, blocking collectives, body(): lax.psum(jnp.sum(exp_scores, axis=-1).astype(jnp.bfloat16), 'token')  124 us
    pmax x1, blocking collectives, body(): lax.pmax(local_max.astype(jnp.bfloat16), 'token').astype(local_max.dtype)  122 us
    all_gather x1, waiting for transfers between devices, body(): lax.all_gather(w_query, 'image', axis=0, tiled=True)  90.2 us
  transfers between devices with their start and end apart: 9, of which 9 were waited for; matrix products, arithmetic and copies ran while one was open for 0% of the time, Pallas kernels for 0%

commit v1 on v0

v1 whole, which is shorter than its diff:
```python
import functools
import math

import jax
import jax.numpy as jnp
from jax import lax
from jax.experimental import pallas as pl
from jax.experimental.pallas import tpu as pltpu
from jax.sharding import PartitionSpec as P

HD = 128
TILE = 128
SIDE = 4
MESH = pl.DeviceIdType.MESH
LOG2E = 1.4426950408889634


def head_chip(head):
    row = head // (SIDE - 1)
    col = (row + 1 + head % (SIDE - 1)) % SIDE
    return row * SIDE + col


def kernel(
    tiles_ref,
    count_ref,
    guide_ref,
    hidden_ref,
    key_ref,
    value_ref,
    w_ref,
    out_ref,
    hid,
    wbuf,
    acc,
    qsend,
    qbuf,
    kbuf,
    vbuf,
    score,
    attended,
    other,
    guided,
    osend,
    local_sem,
    hid_sem,
    w_send,
    w_recv,
    kv_send,
    kv_recv,
    q_send,
    q_recv,
    x_sem,
    o_send,
    o_recv,
):
    image = lax.axis_index("image")
    token = lax.axis_index("token")
    images = hidden_ref.shape[3] // w_ref.shape[0]
    core = lax.rem(token, 2)
    chip = token // 2
    partner = token + 1 - 2 * core
    row = chip // SIDE
    col = lax.rem(chip, SIDE)
    turn = lax.rem(col - row - 1 + 2 * SIDE, SIDE)
    has_head = turn < SIDE - 1
    my_head = jnp.minimum(row * (SIDE - 1) + turn, 11)
    token_count = 2 * SIDE * SIDE
    heads = key_ref.shape[3] // HD
    half_heads = heads // 2
    depth = w_ref.shape[0]
    half_cols = w_ref.shape[1] // 2
    slots = tiles_ref.shape[1]
    up = lax.rem(image + 1, images)
    down = lax.rem(image + images - 1, images)

    my_cols = pl.ds(pl.multiple_of(core * half_cols, 128), half_cols)
    w_own = pltpu.make_async_copy(w_ref.at[:, my_cols], wbuf.at[0], local_sem.at[0])
    w_own.start()
    hid_own = pltpu.make_async_copy(hidden_ref.at[:, 0], hid.at[:, core], local_sem.at[1])
    hid_own.start()

    barrier = pltpu.get_barrier_semaphore()

    @pl.loop(1, token_count)
    def _(step):
        peer = lax.rem(token + step, token_count)
        pl.semaphore_signal(barrier, inc=1, device_id=(image, peer), device_id_type=MESH)

    for near in (up, down):
        pl.semaphore_signal(barrier, inc=1, device_id=(near, token), device_id_type=MESH)
    pl.semaphore_wait(barrier, token_count - 1 + 2)

    half = depth // 2
    first, second = pl.ds(0, half), pl.ds(half, half)

    def w_copy(index, src, slot, rows, near):
        return pltpu.make_async_remote_copy(
            src_ref=src,
            dst_ref=wbuf.at[slot, rows],
            send_sem=w_send.at[index],
            recv_sem=w_recv.at[index],
            device_id=(near, token),
            device_id_type=MESH,
        )

    up_first = w_copy(0, w_ref.at[first, my_cols], 1, first, up)
    down_second = w_copy(1, w_ref.at[second, my_cols], 2, second, down)
    up_second = w_copy(2, w_ref.at[second, my_cols], 1, second, up)
    down_first = w_copy(3, w_ref.at[first, my_cols], 2, first, down)
    up_relay = w_copy(4, wbuf.at[1, first], 3, first, up)
    down_relay = w_copy(5, wbuf.at[2, second], 3, second, down)
    for copy in (up_first, down_second, up_second, down_first):
        copy.start()

    hid_out = pltpu.make_async_remote_copy(
        src_ref=hidden_ref.at[:, 0],
        dst_ref=hid.at[:, core],
        send_sem=hid_sem.at[0],
        recv_sem=hid_sem.at[1],
        device_id=(image, partner),
        device_id_type=MESH,
    )
    hid_out.start()

    def kv_pair(step):
        branch = lax.rem(step, 2)
        head = lax.rem(my_head + step // 2, heads)
        target = head_chip(head) * 2 + branch
        lanes = pl.ds(pl.multiple_of(head * HD, HD), HD)
        pairs = (
            (key_ref.at[branch, 0, :, lanes], kbuf.at[token], 0),
            (value_ref.at[branch, 0, :, lanes], vbuf.at[token], 1),
        )
        return target, pairs

    def kv_remote(step, target, src, dst, kind):
        return pltpu.make_async_remote_copy(
            src_ref=src,
            dst_ref=dst,
            send_sem=kv_send.at[kind, step],
            recv_sem=kv_recv.at[kind],
            device_id=(image, target),
            device_id_type=MESH,
        )

    @pl.loop(0, 2 * heads)
    def _(step):
        target, pairs = kv_pair(step)

        @pl.when(target != token)
        def _():
            for src, dst, kind in pairs:
                kv_remote(step, target, src, dst, kind).start()

        @pl.when(target == token)
        def _():
            for src, dst, kind in pairs:
                pltpu.make_async_copy(src, dst, kv_recv.at[kind]).start()

    rows_all = 4 * TILE
    width = 256

    def project(slot, owner, start, size, is_first):
        features = pl.ds(pl.multiple_of(owner * depth + start, 128), size)

        @pl.loop(0, half_cols // width)
        def _(step):
            cols = pl.ds(pl.multiple_of(step * width, width), width)
            part = jnp.dot(
                hid[:, :, :, features].reshape(rows_all, size),
                wbuf[slot, pl.ds(start, size), cols],
                preferred_element_type=jnp.float32,
            )
            if is_first:
                acc[:, cols] = part
            else:
                acc[:, cols] += part

    far = lax.rem(image + 2, images)
    w_own.wait()
    hid_own.wait()
    hid_out.wait_recv()
    project(0, image, 0, depth, True)
    up_first.wait_recv()
    up_relay.start()
    down_second.wait_recv()
    down_relay.start()
    project(1, down, 0, half, False)
    project(2, up, half, half, False)
    up_second.wait_recv()
    project(1, down, half, half, False)
    down_first.wait_recv()
    project(2, up, 0, half, False)
    up_relay.wait_recv()
    project(3, far, 0, half, False)
    down_relay.wait_recv()
    project(3, far, half, half, False)

    for head in range(half_heads):
        block = acc[:, head * HD : (head + 1) * HD].astype(jnp.bfloat16)
        qsend[:, head] = block.reshape(2, 2, TILE, HD)

    def q_where(step):
        branch = lax.rem(step, 2)
        local_head = lax.rem(my_head + step // 2, half_heads)
        target = head_chip(core * half_heads + local_head) * 2 + branch
        return target, qsend.at[branch, local_head], qbuf.at[pl.ds(chip * 2, 2)]

    def q_remote(step):
        target, src, dst = q_where(step)
        return pltpu.make_async_remote_copy(
            src_ref=src,
            dst_ref=dst,
            send_sem=q_send.at[step],
            recv_sem=q_recv,
            device_id=(image, target),
            device_id_type=MESH,
        )

    @pl.loop(0, 2 * half_heads)
    def _(step):
        target, src, dst = q_where(step)

        @pl.when(target != token)
        def _():
            q_remote(step).start()

        @pl.when(target == token)
        def _():
            pltpu.make_async_copy(src, dst, q_recv).start()

    share = TILE // 2
    mine_rows = pl.ds(pl.multiple_of(core * share, share), share)
    sent_rows = pl.ds(pl.multiple_of((1 - core) * share, share), share)
    exchange = pltpu.make_async_remote_copy(
        src_ref=attended.at[:, sent_rows],
        dst_ref=other,
        send_sem=x_sem.at[0],
        recv_sem=x_sem.at[1],
        device_id=(image, partner),
        device_id_type=MESH,
    )

    def o_where(target):
        lanes = pl.ds(pl.multiple_of(my_head * HD, HD), HD)
        return osend.at[target], out_ref.at[mine_rows, lanes]

    def o_remote(target):
        src, dst = o_where(target)
        return pltpu.make_async_remote_copy(
            src_ref=src,
            dst_ref=dst,
            send_sem=o_send.at[target],
            recv_sem=o_recv,
            device_id=(image, target),
            device_id_type=MESH,
        )

    @pl.when(has_head)
    def _():
        pltpu.make_async_copy(kbuf, kbuf, kv_recv.at[0]).wait()
        pltpu.make_async_copy(vbuf, vbuf, kv_recv.at[1]).wait()
        pltpu.make_async_copy(qbuf, qbuf, q_recv).wait()
        factor = LOG2E / math.sqrt(HD)
        span = 8
        chunk = span * TILE
        chunks = token_count // span

        @pl.loop(0, slots // 2)
        def _(pair):
            query = jnp.concatenate(
                [qbuf[tiles_ref[0, 2 * pair]], qbuf[tiles_ref[0, 2 * pair + 1]]], axis=0
            )
            peak = jnp.full((2 * TILE, 128), -jnp.inf, jnp.float32)
            for part in range(chunks):
                keys = kbuf[part * span : (part + 1) * span].reshape(chunk, HD)
                logits = lax.dot_general(
                    query, keys, (((1,), (1,)), ((), ())), preferred_element_type=jnp.float32
                )
                score[:, part * chunk : (part + 1) * chunk] = logits
                for piece in range(span):
                    peak = jnp.maximum(peak, logits[:, piece * 128 : (piece + 1) * 128])
            top = jnp.max(peak, axis=-1, keepdims=True) * factor
            total = jnp.zeros((2 * TILE, 128), jnp.float32)
            summed = jnp.zeros((2 * TILE, HD), jnp.float32)
            for part in range(chunks):
                values = vbuf[part * span : (part + 1) * span].reshape(chunk, HD)
                weight = jnp.exp2(score[:, part * chunk : (part + 1) * chunk] * factor - top)
                for piece in range(span):
                    total = total + weight[:, piece * 128 : (piece + 1) * 128]
                summed = summed + jnp.dot(
                    weight.astype(jnp.bfloat16), values, preferred_element_type=jnp.float32
                )
            summed = summed / jnp.sum(total, axis=-1, keepdims=True)
            attended[pl.ds(2 * pair, 2)] = summed.reshape(2, TILE, HD)

        exchange.start()
        exchange.wait_recv()
        scale = guide_ref[0]
        mine = attended[:, mine_rows]
        theirs = other[...]
        cond = jnp.where(core == 0, mine, theirs)
        uncond = jnp.where(core == 0, theirs, mine)
        guided[...] = (uncond + scale * (cond - uncond)).astype(jnp.bfloat16)

        @pl.loop(0, token_count)
        def _(target):
            slot = jnp.int32(0)
            for j in range(slots):
                slot = jnp.where(
                    (tiles_ref[0, j] == target) & (count_ref[0] > j), jnp.int32(j), slot
                )
            osend[target] = guided[slot]

        @pl.loop(0, token_count)
        def _(step):
            target = lax.rem(token + step, token_count)

            @pl.when(target != token)
            def _():
                o_remote(target).start()

            @pl.when(target == token)
            def _():
                src, dst = o_where(target)
                pltpu.make_async_copy(src, dst, o_recv).start()

    for copy in (up_first, down_second, up_second, down_first, up_relay, down_relay, hid_out):
        copy.wait_send()

    @pl.loop(0, 2 * heads)
    def _(step):
        target, pairs = kv_pair(step)

        @pl.when(target != token)
        def _():
            for src, dst, kind in pairs:
                kv_remote(step, target, src, dst, kind).wait_send()

    @pl.loop(0, 2 * half_heads)
    def _(step):
        target, _, _ = q_where(step)

        @pl.when(target != token)
        def _():
            q_remote(step).wait_send()

    @pl.when(has_head)
    def _():
        exchange.wait_send()

        @pl.loop(0, token_count)
        def _(target):
            @pl.when(target != token)
            def _():
                o_remote(target).wait_send()

    pltpu.make_async_copy(out_ref, out_ref, o_recv).wait()


def attend(hidden, key_cache, value_cache, w_query, guide, masked_tiles, mask_count):
    tokens = 2 * SIDE * SIDE
    inner = key_cache.shape[3]
    heads = inner // HD
    slots = masked_tiles.shape[1]
    width = hidden.shape[3]
    images = width // w_query.shape[0]
    dma = pltpu.SemaphoreType.DMA
    return pl.pallas_call(
        kernel,
        out_shape=jax.ShapeDtypeStruct((TILE, inner), jnp.bfloat16),
        in_specs=[pl.BlockSpec(memory_space=pltpu.SMEM)] * 3
        + [pl.BlockSpec(memory_space=pl.ANY)] * 4,
        out_specs=pl.BlockSpec(memory_space=pltpu.VMEM),
        scratch_shapes=[
            pltpu.VMEM((2, 2, TILE, width), jnp.bfloat16),
            pltpu.VMEM((images, w_query.shape[0], inner // 2), jnp.bfloat16),
            pltpu.VMEM((4 * TILE, inner // 2), jnp.float32),
            pltpu.VMEM((2, heads // 2, 2, TILE, HD), jnp.bfloat16),
            pltpu.VMEM((tokens, TILE, HD), jnp.bfloat16),
            pltpu.VMEM((tokens, TILE, HD), jnp.bfloat16),
            pltpu.VMEM((tokens, TILE, HD), jnp.bfloat16),
            pltpu.VMEM((2 * TILE, tokens * TILE), jnp.float32),
            pltpu.VMEM((slots, TILE, HD), jnp.float32),
            pltpu.VMEM((slots, TILE // 2, HD), jnp.float32),
            pltpu.VMEM((slots, TILE // 2, HD), jnp.bfloat16),
            pltpu.VMEM((tokens, TILE // 2, HD), jnp.bfloat16),
            dma((2,)),
            dma((2,)),
            dma((6,)),
            dma((6,)),
            dma((2, 2 * heads)),
            dma((2,)),
            dma((heads,)),
            dma,
            dma((2,)),
            dma((tokens,)),
            dma,
        ],
        compiler_params=pltpu.CompilerParams(
            collective_id=0, has_side_effects=True, vmem_limit_bytes=60 * 1024 * 1024
        ),
    )(masked_tiles, mask_count, guide, hidden, key_cache, value_cache, w_query)


def body(hidden, key_cache, value_cache, cached_out, w_query, guide, masked_tiles, mask_count):
    rows = attend(hidden, key_cache, value_cache, w_query, guide, masked_tiles, mask_count)
    token = lax.axis_index("token")
    used = jnp.arange(masked_tiles.shape[1], dtype=jnp.int32) < mask_count[0]
    pasted = jnp.any((masked_tiles[0] == token) & used)
    return jnp.where(pasted, rows[None], cached_out)


def solution(mesh):
    return jax.shard_map(
        body,
        mesh=mesh,
        in_specs=(
            P(None, "image", "token", None),
            P(None, "image", "token", None),
            P(None, "image", "token", None),
            P("image", "token", None),
            P("image", None),
            P("image"),
            P("image", None),
            P("image"),
        ),
        out_specs=P("image", "token", None),
        check_vma=False,
    )
```

time: 1480 us -> 91.1 us (0.06)
  waiting for transfers between devices: 939 us -> 0 us
  blocking collectives: 397 us -> 0 us
  Pallas kernels: 0 us -> 85.8 us
  local copies, waits for them, and re-layouts: 56 us -> 0.01 us
  matrix products: 28.5 us -> 0 us
  other arithmetic: 29.6 us -> 3.77 us
    psum x8 -> x0, waiting for transfers between devices: 848 us -> none  [spread(): return lax.psum(jnp.where(mine, array, jnp.zeros_like(array)), axis)]
    psum x2 -> x0, blocking collectives: 275 us -> none  [the longest x1 151 us: body(): summed_rows = lax.psum(guided_part, 'token')]
    pmax x1 -> x0, blocking collectives: 122 us -> none  [body(): lax.pmax(local_max.astype(jnp.bfloat16), 'token').astype(local_max.dtype)]
    all_gather x1 -> x0, waiting for transfers between devices: 90.2 us -> none  [body(): lax.all_gather(w_query, 'image', axis=0, tiled=True)]
    pallas_call x0 -> x1, Pallas kernels: none -> 85.8 us  [attend(): pl.pallas_call(kernel, out_shape=jax.ShapeDtypeStruct((TILE, inner), jnp....]
    dot_general x4 -> x0, matrix products: 28.5 us -> none  [the longest x1 12 us: body(): jnp.einsum('bimhrk,bikhd->bimrhd', softmax_weights, value_block, preferre...]
    slice x3 -> x0, local copies, waits for them, and re-layouts: 24.5 us -> none  [body(): guided_part = attended[1] + guide_scale * (attended[0] - attended[1])]
    dynamic_update_slice x16 -> x0, local copies, waits for them, and re-layouts: 19.7 us -> none  [send_one(): return lax.dynamic_update_index_in_dim(gathered, arrived, slot_index, 1)]
  transfers between devices with their start and end apart: 9 -> 0, of which waited for: 9 -> 0; matrix products, arithmetic and copies ran while one was open for 0% -> 0% of each run, Pallas kernels for 0% -> 0%
where the time goes in v1:
time: 91.1 us; the launch traced here: 90.9 us
  Pallas kernels  85.8 us (94%)
  other arithmetic  3.77 us (4%)
  between operations  1.31 us (1%)
    pallas_call x1, Pallas kernels, attend(): pl.pallas_call(kernel, out_shape=jax.ShapeDtypeStruct((TILE, inner), jnp....  85.8 us
    select_n x1, other arithmetic, body(): return jnp.where(pasted, rows[None], cached_out)  2.41 us

profile of v1, /device:TPU:1, one launch (start us, length us, event | category | flops | bytes accessed | tf_op | source)
XLA Modules:
  0.0 90.9 jit_solution(785570584960070406)
XLA Ops:
  1.3 1.4 %fusion = pred[]{:T(512)} fusion(s32[1,8]{1,0:T(1,128)} %tiles_ref.1, s32[]{:T(128)} %bitcast.7, s32[]{:T(128)S(6)} %axis_index.12), kind=kLoop, calls=%fused_computation.2 | loop fusion | flops 31 | bytes 41 | tf_op jit(solution)/shard_map/reduce_or | solution.py:411
  2.7 0.0 copy-start
  2.7 85.8 %shard_map.82 = bf16[128,1536]{1,0:T(8,128)(2,1)} custom-call(s32[1,8]{1,0:T(1,128)} %tiles_ref.1, s32[1]{0:T(128)} %copy.10.count_ref, f32[1]{0:T(128)S(6)} %copy.9.guide_ref, bf16[2,1,128,3072]{3,2,1,0:T(8,128)(2,1)} %hidden_ref.1, bf16[2,1,128,1536]{3,2,1,0:T(8,128)(2,1)} %key_ref.1, bf16[2,1,128,1536]{3,2,1,0:T(8,128)(2,1)} %value_ref.1, ...), custom_call_target="tpu_custom_call" | custom-call | tf_op jit(solution)/shard_map/pallas_call | solution.py:370
  88.5 0.0 copy-done
  88.5 2.4 %bitcast_select_fusion = bf16[1,128,1536]{2,1,0:T(8,128)(2,1)} fusion(bf16[1,128,1536]{2,1,0:T(8,128)(2,1)S(1)} %copy-done, bf16[128,1536]{1,0:T(8,128)(2,1)} %shard_map.82, pred[]{:T(512)} %fusion), kind=kLoop, calls=%fused_computation | loop fusion | flops 196608 | bytes 1179649 | tf_op jit(solution)/shard_map/jit(_where)/select_n | solution.py:412
Async XLA Ops:
  2.7 85.8 %copy-start = (bf16[1,128,1536]{2,1,0:T(8,128)(2,1)S(1)}, bf16[1,128,1536]{2,1,0:T(8,128)(2,1)}, u32[]{:S(2)}) copy-start(bf16[1,128,1536]{2,1,0:T(8,128)(2,1)} %param.11) | copy-start | bytes 1179652

commit v2 on v1

v2 whole, which is shorter than its diff:
```python
import functools
import math

import jax
import jax.numpy as jnp
from jax import lax
from jax.experimental import pallas as pl
from jax.experimental.pallas import tpu as pltpu
from jax.sharding import PartitionSpec as P

HD = 128
TILE = 128
SIDE = 4
STAGES = 4
PARTS = 3
MESH = pl.DeviceIdType.MESH
LOG2E = 1.4426950408889634


def head_of(row, col):
    turn = lax.rem(col - row - 1 + 2 * SIDE, SIDE)
    last = SIDE - 2
    return row * (SIDE - 1) + jnp.minimum(turn, last), turn <= last


def offset_chip(row, col, step):
    turn = step // SIDE
    to_row = lax.rem(row + 2 * turn + step, SIDE)
    to_col = lax.rem(col + 3 * turn + step, SIDE)
    return to_row, to_col


def kernel(
    tiles_ref,
    count_ref,
    guide_ref,
    hidden_ref,
    key_ref,
    value_ref,
    w_ref,
    out_ref,
    hid,
    wbuf,
    acc,
    qsend,
    qbuf,
    qnow,
    kbuf,
    vbuf,
    score,
    attended,
    other,
    guided,
    osend,
    slot_of,
    local_sem,
    hid_sem,
    w_send,
    w_recv,
    kv_send,
    kv_recv,
    q_send,
    q_recv,
    x_send,
    x_recv,
    o_send,
    o_recv,
):
    image = lax.axis_index("image")
    token = lax.axis_index("token")
    images = hidden_ref.shape[3] // w_ref.shape[0]
    core = lax.rem(token, 2)
    chip = token // 2
    partner = token + 1 - 2 * core
    row = chip // SIDE
    col = lax.rem(chip, SIDE)
    my_head, has_head = head_of(row, col)
    odd = lax.rem(col, 2)
    right = (row * SIDE + lax.rem(col + 1, SIDE)) * 2 + core
    left = (row * SIDE + lax.rem(col + SIDE - 1, SIDE)) * 2 + core
    token_count = 2 * SIDE * SIDE
    heads = key_ref.shape[3] // HD
    half_heads = heads // 2
    depth = w_ref.shape[0]
    half_cols = w_ref.shape[1] // 2
    slots = tiles_ref.shape[1]
    up = lax.rem(image + 1, images)
    down = lax.rem(image + images - 1, images)

    my_cols = pl.ds(pl.multiple_of(core * half_cols, 128), half_cols)
    w_own = pltpu.make_async_copy(w_ref.at[:, my_cols], wbuf.at[0], local_sem.at[0])
    w_own.start()
    hid_own = pltpu.make_async_copy(hidden_ref.at[:, 0], hid.at[:, core], local_sem.at[1])
    hid_own.start()

    barrier = pltpu.get_barrier_semaphore()

    @pl.loop(1, token_count)
    def _(step):
        peer = lax.rem(token + step, token_count)
        pl.semaphore_signal(barrier, inc=1, device_id=(image, peer), device_id_type=MESH)

    for near in (up, down):
        pl.semaphore_signal(barrier, inc=1, device_id=(near, token), device_id_type=MESH)
    pl.semaphore_wait(barrier, token_count - 1 + 2)

    half = depth // 2
    piece = half // PARTS
    early_1, early_2 = 1 - odd, odd

    def w_rows(part, k):
        return pl.ds(pl.multiple_of(part * half + k * piece, 128), piece)

    def w_copy(index, src, slot, part, k, to_image, to_token):
        return pltpu.make_async_remote_copy(
            src_ref=src,
            dst_ref=wbuf.at[slot, w_rows(part, k)],
            send_sem=w_send.at[index, k],
            recv_sem=w_recv.at[slot - 1, part, k],
            device_id=(to_image, to_token),
            device_id_type=MESH,
        )

    def w_direct(index, slot, part, k):
        near = up if slot == 1 else down
        return w_copy(index, w_ref.at[w_rows(part, k), my_cols], slot, part, k, near, token)

    def w_pass(index, slot, part, k, new_slot, to_image, to_token):
        src = wbuf.at[slot, w_rows(part, k)]
        return w_copy(index, src, new_slot, part, k, to_image, to_token)

    def w_wait(slot, part, k):
        dst = wbuf.at[slot, w_rows(part, k)]
        pltpu.make_async_copy(dst, dst, w_recv.at[slot - 1, part, k]).wait()

    def direct_early(k):
        return w_direct(0, 1, early_1, k), w_direct(1, 2, early_2, k)

    def direct_late(k):
        return w_direct(2, 1, 0, k), w_direct(3, 2, 1, k)

    def pass_early(k):
        to_1 = jnp.where(odd == 1, token, right)
        to_2 = jnp.where(odd == 1, token, left)
        return (
            w_pass(4, 1, early_1, k, 1 + 2 * odd, jnp.where(odd == 1, up, image), to_1),
            w_pass(5, 2, early_2, k, 2 + odd, jnp.where(odd == 1, down, image), to_2),
        )

    def pass_late(k):
        return w_pass(2, 3, 0, k, 3, image, right), w_pass(3, 3, 1, k, 3, image, left)

    for k in range(PARTS):
        for copy in direct_early(k):
            copy.start()

    @pl.when(odd == 0)
    def _():
        for k in range(PARTS):
            for copy in direct_late(k):
                copy.start()

    hid_out = pltpu.make_async_remote_copy(
        src_ref=hidden_ref.at[:, 0],
        dst_ref=hid.at[:, core],
        send_sem=hid_sem.at[0],
        recv_sem=hid_sem.at[1],
        device_id=(image, partner),
        device_id_type=MESH,
    )
    hid_out.start()

    def kv_pair(step):
        branch = lax.rem(step, 2)
        to_row, to_col = offset_chip(row, col, step // 2)
        head, there = head_of(to_row, to_col)
        target = (to_row * SIDE + to_col) * 2 + branch
        lanes = pl.ds(pl.multiple_of(head * HD, HD), HD)
        pairs = (
            (key_ref.at[branch, 0, :, lanes], kbuf.at[token], 0),
            (value_ref.at[branch, 0, :, lanes], vbuf.at[token], 1),
        )
        return target, there, pairs

    def kv_remote(step, target, src, dst, kind):
        return pltpu.make_async_remote_copy(
            src_ref=src,
            dst_ref=dst,
            send_sem=kv_send.at[kind, step],
            recv_sem=kv_recv.at[kind],
            device_id=(image, target),
            device_id_type=MESH,
        )

    @pl.loop(0, token_count)
    def _(step):
        target, there, pairs = kv_pair(step)

        @pl.when(there & (target != token))
        def _():
            for src, dst, kind in pairs:
                kv_remote(step, target, src, dst, kind).start()

        @pl.when(there & (target == token))
        def _():
            for src, dst, kind in pairs:
                pltpu.make_async_copy(src, dst, kv_recv.at[kind]).start()

    @pl.loop(0, token_count)
    def _(tile):
        slot = jnp.int32(0)
        for j in range(slots):
            hit = (tiles_ref[0, j] == tile) & (count_ref[0] > j)
            slot = jnp.where(hit, jnp.int32(j), slot)
        slot_of[tile] = slot

    rows_all = 4 * TILE
    width = 256

    def project(slot, owner, start, size, is_first):
        features = pl.ds(pl.multiple_of(owner * depth + start, 128), size)
        w_part = pl.ds(pl.multiple_of(start, 128), size)

        @pl.loop(0, half_cols // width)
        def _(step):
            cols = pl.ds(pl.multiple_of(step * width, width), width)
            part = jnp.dot(
                hid[:, :, :, features].reshape(rows_all, size),
                wbuf[slot, w_part, cols],
                preferred_element_type=jnp.float32,
            ).reshape(2, 2, TILE, width)
            if is_first:
                acc[:, :, :, cols] = part
            else:
                acc[:, :, :, cols] += part

    far = lax.rem(image + 2, images)
    w_own.wait()
    hid_own.wait()
    hid_out.wait_recv()
    project(0, image, 0, depth, True)
    for k in range(PARTS):
        first, second = pass_early(k)
        w_wait(1, early_1, k)
        first.start()
        w_wait(2, early_2, k)
        second.start()
    project(1, down, early_1 * half, half, False)
    project(2, up, early_2 * half, half, False)

    @pl.when(odd == 1)
    def _():
        for k in range(PARTS):
            first, second = pass_late(k)
            w_wait(3, 0, k)
            first.start()
            w_wait(3, 1, k)
            second.start()

    for k in range(PARTS):
        w_wait(1, 1 - early_1, k)
    project(1, down, (1 - early_1) * half, half, False)
    for k in range(PARTS):
        w_wait(2, 1 - early_2, k)
    project(2, up, (1 - early_2) * half, half, False)

    @pl.when(odd == 0)
    def _():
        for k in range(PARTS):
            w_wait(3, 0, k)
            w_wait(3, 1, k)

    project(3, far, 0, depth, False)

    rows = TILE // STAGES

    def q_where(stage, step):
        branch = lax.rem(step, 2)
        to_row, to_col = offset_chip(row, col, step // 2)
        head, there = head_of(to_row, to_col)
        there = there & (head // half_heads == core)
        target = (to_row * SIDE + to_col) * 2 + branch
        src = qsend.at[stage, branch, lax.rem(head, half_heads)]
        return target, there, src, qbuf.at[stage, pl.ds(chip * 2, 2)]

    def q_remote(stage, step):
        target, _, src, dst = q_where(stage, step)
        return pltpu.make_async_remote_copy(
            src_ref=src,
            dst_ref=dst,
            send_sem=q_send.at[stage, step],
            recv_sem=q_recv.at[stage],
            device_id=(image, target),
            device_id_type=MESH,
        )

    for stage in range(STAGES):
        for head in range(half_heads):
            block = acc[:, :, stage * rows : (stage + 1) * rows, head * HD : (head + 1) * HD]
            qsend[stage, :, head] = block.astype(jnp.bfloat16)

        @pl.loop(0, token_count)
        def _(step):
            target, there, src, dst = q_where(stage, step)

            @pl.when(there & (target != token))
            def _():
                q_remote(stage, step).start()

            @pl.when(there & (target == token))
            def _():
                pltpu.make_async_copy(src, dst, q_recv.at[stage]).start()

    share = rows // 2
    mine_rows = pl.ds(pl.multiple_of(core * share, share), share)
    sent_rows = pl.ds(pl.multiple_of((1 - core) * share, share), share)
    factor = LOG2E / math.sqrt(HD)
    span = 8
    chunk = span * TILE
    chunks = token_count // span
    height = slots * rows

    def exchange(stage):
        return pltpu.make_async_remote_copy(
            src_ref=attended.at[stage, :, sent_rows],
            dst_ref=other.at[stage],
            send_sem=x_send.at[stage],
            recv_sem=x_recv.at[stage],
            device_id=(image, partner),
            device_id_type=MESH,
        )

    def o_where(stage, target):
        lanes = pl.ds(pl.multiple_of(my_head * HD, HD), HD)
        put = pl.ds(pl.multiple_of(stage * rows + core * share, share), share)
        return osend.at[stage, target], out_ref.at[put, lanes]

    def o_remote(stage, target):
        src, dst = o_where(stage, target)
        return pltpu.make_async_remote_copy(
            src_ref=src,
            dst_ref=dst,
            send_sem=o_send.at[stage, target],
            recv_sem=o_recv,
            device_id=(image, target),
            device_id_type=MESH,
        )

    def attention(stage):
        qnow[...] = qbuf[stage]
        query = jnp.concatenate([qnow[tiles_ref[0, j]] for j in range(slots)], axis=0)
        peak = jnp.full((height, 128), -jnp.inf, jnp.float32)
        for part in range(chunks):
            keys = kbuf[part * span : (part + 1) * span].reshape(chunk, HD)
            logits = lax.dot_general(
                query, keys, (((1,), (1,)), ((), ())), preferred_element_type=jnp.float32
            )
            score[:, part * chunk : (part + 1) * chunk] = logits
            for lane in range(span):
                peak = jnp.maximum(peak, logits[:, lane * 128 : (lane + 1) * 128])
        top = jnp.max(peak, axis=-1, keepdims=True) * factor
        total = jnp.zeros((height, 128), jnp.float32)
        summed = jnp.zeros((height, HD), jnp.float32)
        for part in range(chunks):
            values = vbuf[part * span : (part + 1) * span].reshape(chunk, HD)
            weight = jnp.exp2(score[:, part * chunk : (part + 1) * chunk] * factor - top)
            for lane in range(span):
                total = total + weight[:, lane * 128 : (lane + 1) * 128]
            summed = summed + jnp.dot(
                weight.astype(jnp.bfloat16), values, preferred_element_type=jnp.float32
            )
        summed = summed / jnp.sum(total, axis=-1, keepdims=True)
        attended[stage] = summed.reshape(slots, rows, HD)

    def deliver(stage):
        exchange(stage).wait_recv()
        scale = guide_ref[0]
        mine = attended[stage, :, mine_rows]
        theirs = other[stage]
        cond = jnp.where(core == 0, mine, theirs)
        uncond = jnp.where(core == 0, theirs, mine)
        guided[stage] = (uncond + scale * (cond - uncond)).astype(jnp.bfloat16)

        @pl.loop(0, token_count)
        def _(tile):
            osend[stage, tile] = guided[stage, slot_of[tile]]

        @pl.loop(0, token_count)
        def _(step):
            to_row, to_col = offset_chip(row, col, step // 2)
            target = (to_row * SIDE + to_col) * 2 + lax.rem(step, 2)

            @pl.when(target != token)
            def _():
                o_remote(stage, target).start()

            @pl.when(target == token)
            def _():
                src, dst = o_where(stage, target)
                pltpu.make_async_copy(src, dst, o_recv).start()

    @pl.when(has_head)
    def _():
        pltpu.make_async_copy(kbuf, kbuf, kv_recv.at[0]).wait()
        pltpu.make_async_copy(vbuf, vbuf, kv_recv.at[1]).wait()

        @pl.loop(0, STAGES)
        def _(stage):
            pltpu.make_async_copy(qbuf.at[stage], qbuf.at[stage], q_recv.at[stage]).wait()
            attention(stage)
            exchange(stage).start()

            @pl.when(stage > 0)
            def _():
                deliver(stage - 1)

        deliver(STAGES - 1)

    hid_out.wait_send()
    for k in range(PARTS):
        for copy in direct_early(k) + pass_early(k):
            copy.wait_send()

    @pl.when(odd == 0)
    def _():
        for k in range(PARTS):
            for copy in direct_late(k):
                copy.wait_send()

    @pl.when(odd == 1)
    def _():
        for k in range(PARTS):
            for copy in pass_late(k):
                copy.wait_send()

    @pl.loop(0, token_count)
    def _(step):
        target, there, pairs = kv_pair(step)

        @pl.when(there & (target != token))
        def _():
            for src, dst, kind in pairs:
                kv_remote(step, target, src, dst, kind).wait_send()

    @pl.loop(0, STAGES)
    def _(stage):
        @pl.loop(0, token_count)
        def _(step):
            target, there, _, _ = q_where(stage, step)

            @pl.when(there & (target != token))
            def _():
                q_remote(stage, step).wait_send()

    @pl.when(has_head)
    def _():
        @pl.loop(0, STAGES)
        def _(stage):
            exchange(stage).wait_send()

            @pl.loop(0, token_count)
            def _(target):
                @pl.when(target != token)
                def _():
                    o_remote(stage, target).wait_send()

    pltpu.make_async_copy(out_ref, out_ref, o_recv).wait()


def attend(hidden, key_cache, value_cache, w_query, guide, masked_tiles, mask_count):
    tokens = 2 * SIDE * SIDE
    inner = key_cache.shape[3]
    heads = inner // HD
    slots = masked_tiles.shape[1]
    width = hidden.shape[3]
    images = width // w_query.shape[0]
    rows = TILE // STAGES
    dma = pltpu.SemaphoreType.DMA
    return pl.pallas_call(
        kernel,
        out_shape=jax.ShapeDtypeStruct((TILE, inner), jnp.bfloat16),
        in_specs=[pl.BlockSpec(memory_space=pltpu.SMEM)] * 3
        + [pl.BlockSpec(memory_space=pl.ANY)] * 4,
        out_specs=pl.BlockSpec(memory_space=pltpu.VMEM),
        scratch_shapes=[
            pltpu.VMEM((2, 2, TILE, width), jnp.bfloat16),
            pltpu.VMEM((images, w_query.shape[0], inner // 2), jnp.bfloat16),
            pltpu.VMEM((2, 2, TILE, inner // 2), jnp.float32),
            pltpu.VMEM((STAGES, 2, heads // 2, 2, rows, HD), jnp.bfloat16),
            pltpu.VMEM((STAGES, tokens, rows, HD), jnp.bfloat16),
            pltpu.VMEM((tokens, rows, HD), jnp.bfloat16),
            pltpu.VMEM((tokens, TILE, HD), jnp.bfloat16),
            pltpu.VMEM((tokens, TILE, HD), jnp.bfloat16),
            pltpu.VMEM((slots * rows, tokens * TILE), jnp.float32),
            pltpu.VMEM((STAGES, slots, rows, HD), jnp.float32),
            pltpu.VMEM((STAGES, slots, rows // 2, HD), jnp.float32),
            pltpu.VMEM((STAGES, slots, rows // 2, HD), jnp.bfloat16),
            pltpu.VMEM((STAGES, tokens, rows // 2, HD), jnp.bfloat16),
            pltpu.SMEM((tokens,), jnp.int32),
            dma((2,)),
            dma((2,)),
            dma((6, PARTS)),
            dma((images - 1, 2, PARTS)),
            dma((2, tokens)),
            dma((2,)),
            dma((STAGES, tokens)),
            dma((STAGES,)),
            dma((STAGES,)),
            dma((STAGES,)),
            dma((STAGES, tokens)),
            dma,
        ],
        compiler_params=pltpu.CompilerParams(
            collective_id=0, has_side_effects=True, vmem_limit_bytes=60 * 1024 * 1024
        ),
    )(masked_tiles, mask_count, guide, hidden, key_cache, value_cache, w_query)


def body(hidden, key_cache, value_cache, cached_out, w_query, guide, masked_tiles, mask_count):
    rows = attend(hidden, key_cache, value_cache, w_query, guide, masked_tiles, mask_count)
    token = lax.axis_index("token")
    used = jnp.arange(masked_tiles.shape[1], dtype=jnp.int32) < mask_count[0]
    pasted = jnp.any((masked_tiles[0] == token) & used)
    return jnp.where(pasted, rows[None], cached_out)


def solution(mesh):
    return jax.shard_map(
        body,
        mesh=mesh,
        in_specs=(
            P(None, "image", "token", None),
            P(None, "image", "token", None),
            P(None, "image", "token", None),
            P("image", "token", None),
            P("image", None),
            P("image"),
            P("image", None),
            P("image"),
        ),
        out_specs=P("image", "token", None),
        check_vma=False,
    )
```

time: 91.1 us -> 90.6 us (level)
  the two profiles are of different devices: /device:TPU:1 before, /device:TPU:27 now
where the time goes in v2:
time: 90.6 us; the launch traced here: 90.4 us
  Pallas kernels  85.3 us (94%)
  other arithmetic  3.77 us (4%)
  between operations  1.31 us (1%)
    pallas_call x1, Pallas kernels, attend(): pl.pallas_call(kernel, out_shape=jax.ShapeDtypeStruct((TILE, inner), jnp....  85.3 us
    select_n x1, other arithmetic, body(): return jnp.where(pasted, rows[None], cached_out)  2.41 us

profile of v2, /device:TPU:27, one launch (start us, length us, event | category | flops | bytes accessed | tf_op | source)
XLA Modules:
  0.0 90.4 jit_solution(11364060423715479432)
XLA Ops:
  1.3 1.4 %fusion = pred[]{:T(512)} fusion(s32[1,8]{1,0:T(1,128)} %tiles_ref.1, s32[]{:T(128)} %bitcast.7, s32[]{:T(128)S(6)} %axis_index.12), kind=kLoop, calls=%fused_computation.2 | loop fusion | flops 31 | bytes 41 | tf_op jit(solution)/shard_map/reduce_or | solution.py:523
  2.7 0.0 copy-start
  2.7 85.3 %shard_map.82 = bf16[128,1536]{1,0:T(8,128)(2,1)} custom-call(s32[1,8]{1,0:T(1,128)} %tiles_ref.1, s32[1]{0:T(128)} %copy.10.count_ref, f32[1]{0:T(128)S(6)} %copy.9.guide_ref, bf16[2,1,128,3072]{3,2,1,0:T(8,128)(2,1)} %hidden_ref.1, bf16[2,1,128,1536]{3,2,1,0:T(8,128)(2,1)} %key_ref.1, bf16[2,1,128,1536]{3,2,1,0:T(8,128)(2,1)} %value_ref.1, ...), custom_call_target="tpu_custom_call" | custom-call | tf_op jit(solution)/shard_map/pallas_call | solution.py:479
  88.0 0.0 copy-done
  88.0 2.4 %bitcast_select_fusion = bf16[1,128,1536]{2,1,0:T(8,128)(2,1)} fusion(bf16[1,128,1536]{2,1,0:T(8,128)(2,1)S(1)} %copy-done, bf16[128,1536]{1,0:T(8,128)(2,1)} %shard_map.82, pred[]{:T(512)} %fusion), kind=kLoop, calls=%fused_computation | loop fusion | flops 196608 | bytes 1179649 | tf_op jit(solution)/shard_map/jit(_where)/select_n | solution.py:524
Async XLA Ops:
  2.7 85.3 %copy-start = (bf16[1,128,1536]{2,1,0:T(8,128)(2,1)S(1)}, bf16[1,128,1536]{2,1,0:T(8,128)(2,1)}, u32[]{:S(2)}) copy-start(bf16[1,128,1536]{2,1,0:T(8,128)(2,1)} %param.11) | copy-start | bytes 1179652

commit v3 on v2

--- a/solution.py
+++ b/solution.py
@@ -12,22 +12,20 @@
 TILE = 128
 SIDE = 4
 STAGES = 4
-PARTS = 3
+PARTS = 6
 MESH = pl.DeviceIdType.MESH
 LOG2E = 1.4426950408889634
 
 
 def head_of(row, col):
-    turn = lax.rem(col - row - 1 + 2 * SIDE, SIDE)
+    turn = (col - row - 1) & (SIDE - 1)
     last = SIDE - 2
     return row * (SIDE - 1) + jnp.minimum(turn, last), turn <= last
 
 
-def offset_chip(row, col, step):
-    turn = step // SIDE
-    to_row = lax.rem(row + 2 * turn + step, SIDE)
-    to_col = lax.rem(col + 3 * turn + step, SIDE)
-    return to_row, to_col
+OFFSETS = tuple(
+    ((2 * (i // SIDE) + i) % SIDE, (3 * (i // SIDE) + i) % SIDE) for i in range(1, SIDE * SIDE)
+)
 
 
 def kernel(
@@ -38,6 +36,7 @@
     key_ref,
     value_ref,
     w_ref,
+    cached_ref,
     out_ref,
     hid,
     wbuf,
@@ -52,6 +51,8 @@
     other,
     guided,
     osend,
+    arrived,
+    cached,
     slot_of,
     local_sem,
     hid_sem,
@@ -69,39 +70,40 @@
     image = lax.axis_index("image")
     token = lax.axis_index("token")
     images = hidden_ref.shape[3] // w_ref.shape[0]
-    core = lax.rem(token, 2)
-    chip = token // 2
-    partner = token + 1 - 2 * core
-    row = chip // SIDE
-    col = lax.rem(chip, SIDE)
+    core = token & 1
+    chip = token >> 1
+    partner = token ^ 1
+    row = chip >> 2
+    col = chip & (SIDE - 1)
     my_head, has_head = head_of(row, col)
-    odd = lax.rem(col, 2)
-    right = (row * SIDE + lax.rem(col + 1, SIDE)) * 2 + core
-    left = (row * SIDE + lax.rem(col + SIDE - 1, SIDE)) * 2 + core
+    odd = col & 1
+    right = (row * SIDE + ((col + 1) & (SIDE - 1))) * 2 + core
+    left = (row * SIDE + ((col - 1) & (SIDE - 1))) * 2 + core
     token_count = 2 * SIDE * SIDE
     heads = key_ref.shape[3] // HD
     half_heads = heads // 2
     depth = w_ref.shape[0]
     half_cols = w_ref.shape[1] // 2
     slots = tiles_ref.shape[1]
-    up = lax.rem(image + 1, images)
-    down = lax.rem(image + images - 1, images)
+    up = (image + 1) & (images - 1)
+    down = (image - 1) & (images - 1)
+    far = image ^ 2
 
     my_cols = pl.ds(pl.multiple_of(core * half_cols, 128), half_cols)
     w_own = pltpu.make_async_copy(w_ref.at[:, my_cols], wbuf.at[0], local_sem.at[0])
     w_own.start()
     hid_own = pltpu.make_async_copy(hidden_ref.at[:, 0], hid.at[:, core], local_sem.at[1])
     hid_own.start()
+    cached_own = pltpu.make_async_copy(cached_ref.at[0], cached, local_sem.at[2])
+    cached_own.start()
 
     barrier = pltpu.get_barrier_semaphore()
-
-    @pl.loop(1, token_count)
-    def _(step):
-        peer = lax.rem(token + step, token_count)
-        pl.semaphore_signal(barrier, inc=1, device_id=(image, peer), device_id_type=MESH)
 
     for near in (up, down):
         pl.semaphore_signal(barrier, inc=1, device_id=(near, token), device_id_type=MESH)
+    for step in range(1, token_count):
+        peer = token ^ step
+        pl.semaphore_signal(barrier, inc=1, device_id=(image, peer), device_id_type=MESH)
     pl.semaphore_wait(barrier, token_count - 1 + 2)
 
     half = depth // 2
@@ -109,7 +111,7 @@
     early_1, early_2 = 1 - odd, odd
 
     def w_rows(part, k):
-        return pl.ds(pl.multiple_of(part * half + k * piece, 128), piece)
+        return pl.ds(pl.multiple_of(part * half + k * piece, piece), piece)
 
     def w_copy(index, src, slot, part, k, to_image, to_token):
         return pltpu.make_async_remote_copy(
@@ -170,41 +172,39 @@
     )
     hid_out.start()
 
-    def kv_pair(step):
-        branch = lax.rem(step, 2)
-        to_row, to_col = offset_chip(row, col, step // 2)
-        head, there = head_of(to_row, to_col)
-        target = (to_row * SIDE + to_col) * 2 + branch
+    def kv_pairs(head, branch):
         lanes = pl.ds(pl.multiple_of(head * HD, HD), HD)
-        pairs = (
+        return (
             (key_ref.at[branch, 0, :, lanes], kbuf.at[token], 0),
             (value_ref.at[branch, 0, :, lanes], vbuf.at[token], 1),
         )
-        return target, there, pairs
-
-    def kv_remote(step, target, src, dst, kind):
-        return pltpu.make_async_remote_copy(
-            src_ref=src,
-            dst_ref=dst,
-            send_sem=kv_send.at[kind, step],
-            recv_sem=kv_recv.at[kind],
-            device_id=(image, target),
-            device_id_type=MESH,
-        )
-
-    @pl.loop(0, token_count)
-    def _(step):
-        target, there, pairs = kv_pair(step)
-
-        @pl.when(there & (target != token))
+
+    def kv_start(head, branch, target):
+        for src, dst, kind in kv_pairs(head, branch):
+            pltpu.make_async_remote_copy(
+                src_ref=src,
+                dst_ref=dst,
+                send_sem=kv_send.at[kind],
+                recv_sem=kv_recv.at[kind],
+                device_id=(image, target),
+                device_id_type=MESH,
+            ).start()
+
+    for down_rows, right_cols in OFFSETS:
+        to_row, to_col = (row + down_rows) & (SIDE - 1), (col + right_cols) & (SIDE - 1)
+        to_head, there = head_of(to_row, to_col)
+        to_chip = to_row * SIDE + to_col
+
+        @pl.when(there)
         def _():
-            for src, dst, kind in pairs:
-                kv_remote(step, target, src, dst, kind).start()
-
-        @pl.when(there & (target == token))
-        def _():
-            for src, dst, kind in pairs:
-                pltpu.make_async_copy(src, dst, kv_recv.at[kind]).start()
+            for branch in range(2):
+                kv_start(to_head, branch, to_chip * 2 + branch)
+
+    @pl.when(has_head)
+    def _():
+        kv_start(my_head, 1 - core, partner)
+        for src, dst, kind in kv_pairs(my_head, core):
+            pltpu.make_async_copy(src, dst, kv_recv.at[kind]).start()
 
     @pl.loop(0, token_count)
     def _(tile):
@@ -234,7 +234,6 @@
             else:
                 acc[:, :, :, cols] += part
 
-    far = lax.rem(image + 2, images)
     w_own.wait()
     hid_own.wait()
     hid_out.wait_recv()
@@ -274,42 +273,41 @@
 
     rows = TILE // STAGES
 
-    def q_where(stage, step):
-        branch = lax.rem(step, 2)
-        to_row, to_col = offset_chip(row, col, step // 2)
-        head, there = head_of(to_row, to_col)
-        there = there & (head // half_heads == core)
-        target = (to_row * SIDE + to_col) * 2 + branch
-        src = qsend.at[stage, branch, lax.rem(head, half_heads)]
-        return target, there, src, qbuf.at[stage, pl.ds(chip * 2, 2)]
-
-    def q_remote(stage, step):
-        target, _, src, dst = q_where(stage, step)
-        return pltpu.make_async_remote_copy(
-            src_ref=src,
-            dst_ref=dst,
-            send_sem=q_send.at[stage, step],
+    def q_start(stage, head, branch, target):
+        pltpu.make_async_remote_copy(
+            src_ref=qsend.at[stage, branch, head - core * half_heads],
+            dst_ref=qbuf.at[stage, pl.ds(chip * 2, 2)],
+            send_sem=q_send,
             recv_sem=q_recv.at[stage],
             device_id=(image, target),
             device_id_type=MESH,
-        )
-
+        ).start()
+
+    owns_head = has_head & (row >> 1 == core)
     for stage in range(STAGES):
         for head in range(half_heads):
             block = acc[:, :, stage * rows : (stage + 1) * rows, head * HD : (head + 1) * HD]
             qsend[stage, :, head] = block.astype(jnp.bfloat16)
 
-        @pl.loop(0, token_count)
-        def _(step):
-            target, there, src, dst = q_where(stage, step)
-
-            @pl.when(there & (target != token))
+        for step in range(2 * SIDE):
+            to_row = 2 * core + ((row + step) & 1)
+            to_col = (col + step + step // SIDE) & (SIDE - 1)
+            to_head, there = head_of(to_row, to_col)
+            to_chip = to_row * SIDE + to_col
+
+            @pl.when(there & (to_chip != chip))
             def _():
-                q_remote(stage, step).start()
-
-            @pl.when(there & (target == token))
-            def _():
-                pltpu.make_async_copy(src, dst, q_recv.at[stage]).start()
+                for branch in range(2):
+                    q_start(stage, to_head, branch, to_chip * 2 + branch)
+
+        @pl.when(owns_head)
+        def _():
+            q_start(stage, my_head, 1 - core, partner)
+            pltpu.make_async_copy(
+                qsend.at[stage, core, my_head - core * half_heads],
+                qbuf.at[stage, pl.ds(chip * 2, 2)],
+                q_recv.at[stage],
+            ).start()
 
     share = rows // 2
     mine_rows = pl.ds(pl.multiple_of(core * share, share), share)
@@ -330,21 +328,21 @@
             device_id_type=MESH,
         )
 
-    def o_where(stage, target):
+    def o_refs(stage, target):
         lanes = pl.ds(pl.multiple_of(my_head * HD, HD), HD)
         put = pl.ds(pl.multiple_of(stage * rows + core * share, share), share)
-        return osend.at[stage, target], out_ref.at[put, lanes]
-
-    def o_remote(stage, target):
-        src, dst = o_where(stage, target)
-        return pltpu.make_async_remote_copy(
+        return osend.at[stage, target], arrived.at[put, lanes]
+
+    def o_start(stage, target):
+        src, dst = o_refs(stage, target)
+        pltpu.make_async_remote_copy(
             src_ref=src,
             dst_ref=dst,
-            send_sem=o_send.at[stage, target],
+            send_sem=o_send,
             recv_sem=o_recv,
             device_id=(image, target),
             device_id_type=MESH,
-        )
+        ).start()
 
     def attention(stage):
         qnow[...] = qbuf[stage]
@@ -381,40 +379,33 @@
         uncond = jnp.where(core == 0, theirs, mine)
         guided[stage] = (uncond + scale * (cond - uncond)).astype(jnp.bfloat16)
 
-        @pl.loop(0, token_count)
-        def _(tile):
+        for tile in range(token_count):
             osend[stage, tile] = guided[stage, slot_of[tile]]
 
-        @pl.loop(0, token_count)
-        def _(step):
-            to_row, to_col = offset_chip(row, col, step // 2)
-            target = (to_row * SIDE + to_col) * 2 + lax.rem(step, 2)
-
-            @pl.when(target != token)
-            def _():
-                o_remote(stage, target).start()
-
-            @pl.when(target == token)
-            def _():
-                src, dst = o_where(stage, target)
-                pltpu.make_async_copy(src, dst, o_recv).start()
+        for down_rows, right_cols in OFFSETS:
+            to_row, to_col = (row + down_rows) & (SIDE - 1), (col + right_cols) & (SIDE - 1)
+            for to_core in range(2):
+                o_start(stage, (to_row * SIDE + to_col) * 2 + to_core)
+        o_start(stage, partner)
+        src, dst = o_refs(stage, token)
+        pltpu.make_async_copy(src, dst, o_recv).start()
 
     @pl.when(has_head)
     def _():
         pltpu.make_async_copy(kbuf, kbuf, kv_recv.at[0]).wait()
         pltpu.make_async_copy(vbuf, vbuf, kv_recv.at[1]).wait()
 
-        @pl.loop(0, STAGES)
+        @pl.loop(0, STAGES + 1)
         def _(stage):
-            pltpu.make_async_copy(qbuf.at[stage], qbuf.at[stage], q_recv.at[stage]).wait()
-            attention(stage)
-            exchange(stage).start()
+            @pl.when(stage < STAGES)
+            def _():
+                pltpu.make_async_copy(qbuf.at[stage], qbuf.at[stage], q_recv.at[stage]).wait()
+                attention(stage)
+                exchange(stage).start()
 
             @pl.when(stage > 0)
             def _():
                 deliver(stage - 1)
-
-        deliver(STAGES - 1)
 
     hid_out.wait_send()
     for k in range(PARTS):
@@ -433,41 +424,40 @@
             for copy in pass_late(k):
                 copy.wait_send()
 
-    @pl.loop(0, token_count)
-    def _(step):
-        target, there, pairs = kv_pair(step)
-
-        @pl.when(there & (target != token))
-        def _():
-            for src, dst, kind in pairs:
-                kv_remote(step, target, src, dst, kind).wait_send()
-
-    @pl.loop(0, STAGES)
-    def _(stage):
-        @pl.loop(0, token_count)
-        def _(step):
-            target, there, _, _ = q_where(stage, step)
-
-            @pl.when(there & (target != token))
-            def _():
-                q_remote(stage, step).wait_send()
+    def sent(ref, sem):
+        pltpu.make_async_copy(ref, ref, sem).wait()
 
     @pl.when(has_head)
     def _():
-        @pl.loop(0, STAGES)
-        def _(stage):
+        sent(kbuf.at[pl.ds(0, 2 * heads - 1)], kv_send.at[0])
+        sent(vbuf.at[pl.ds(0, 2 * heads - 1)], kv_send.at[1])
+        sent(osend.at[:, pl.ds(0, token_count - 1)], o_send)
+        for stage in range(STAGES):
             exchange(stage).wait_send()
 
-            @pl.loop(0, token_count)
-            def _(target):
-                @pl.when(target != token)
-                def _():
-                    o_remote(stage, target).wait_send()
-
-    pltpu.make_async_copy(out_ref, out_ref, o_recv).wait()
-
-
-def attend(hidden, key_cache, value_cache, w_query, guide, masked_tiles, mask_count):
+    @pl.when(jnp.logical_not(has_head))
+    def _():
+        sent(kbuf.at[pl.ds(0, 2 * heads)], kv_send.at[0])
+        sent(vbuf.at[pl.ds(0, 2 * heads)], kv_send.at[1])
+
+    @pl.when(owns_head)
+    def _():
+        sent(qbuf.at[:, pl.ds(0, 4 * half_heads - 2)], q_send)
+
+    @pl.when(jnp.logical_not(owns_head))
+    def _():
+        sent(qbuf.at[:, pl.ds(0, 4 * half_heads)], q_send)
+
+    pasted = jnp.int32(0)
+    for j in range(slots):
+        hit = (tiles_ref[0, j] == token) & (count_ref[0] > j)
+        pasted = jnp.where(hit, jnp.int32(1), pasted)
+    cached_own.wait()
+    pltpu.make_async_copy(arrived, arrived, o_recv).wait()
+    out_ref[0] = jnp.where(pasted == 1, arrived[...], cached[...])
+
+
+def body(hidden, key_cache, value_cache, cached_out, w_query, guide, masked_tiles, mask_count):
     tokens = 2 * SIDE * SIDE
     inner = key_cache.shape[3]
     heads = inner // HD
@@ -478,9 +468,9 @@
     dma = pltpu.SemaphoreType.DMA
     return pl.pallas_call(
         kernel,
-        out_shape=jax.ShapeDtypeStruct((TILE, inner), jnp.bfloat16),
+        out_shape=jax.ShapeDtypeStruct((1, TILE, inner), jnp.bfloat16),
         in_specs=[pl.BlockSpec(memory_space=pltpu.SMEM)] * 3
-        + [pl.BlockSpec(memory_space=pl.ANY)] * 4,
+        + [pl.BlockSpec(memory_space=pl.ANY)] * 5,
         out_specs=pl.BlockSpec(memory_space=pltpu.VMEM),
         scratch_shapes=[
             pltpu.VMEM((2, 2, TILE, width), jnp.bfloat16),
@@ -496,32 +486,26 @@
             pltpu.VMEM((STAGES, slots, rows // 2, HD), jnp.float32),
             pltpu.VMEM((STAGES, slots, rows // 2, HD), jnp.bfloat16),
             pltpu.VMEM((STAGES, tokens, rows // 2, HD), jnp.bfloat16),
+            pltpu.VMEM((TILE, inner), jnp.bfloat16),
+            pltpu.VMEM((TILE, inner), jnp.bfloat16),
             pltpu.SMEM((tokens,), jnp.int32),
-            dma((2,)),
+            dma((3,)),
             dma((2,)),
             dma((6, PARTS)),
             dma((images - 1, 2, PARTS)),
-            dma((2, tokens)),
             dma((2,)),
-            dma((STAGES, tokens)),
+            dma((2,)),
+            dma,
             dma((STAGES,)),
             dma((STAGES,)),
             dma((STAGES,)),
-            dma((STAGES, tokens)),
+            dma,
             dma,
         ],
         compiler_params=pltpu.CompilerParams(
             collective_id=0, has_side_effects=True, vmem_limit_bytes=60 * 1024 * 1024
         ),
-    )(masked_tiles, mask_count, guide, hidden, key_cache, value_cache, w_query)
-
-
-def body(hidden, key_cache, value_cache, cached_out, w_query, guide, masked_tiles, mask_count):
-    rows = attend(hidden, key_cache, value_cache, w_query, guide, masked_tiles, mask_count)
-    token = lax.axis_index("token")
-    used = jnp.arange(masked_tiles.shape[1], dtype=jnp.int32) < mask_count[0]
-    pasted = jnp.any((masked_tiles[0] == token) & used)
-    return jnp.where(pasted, rows[None], cached_out)
+    )(masked_tiles, mask_count, guide, hidden, key_cache, value_cache, w_query, cached_out)
 
 
 def solution(mesh):

time: 90.6 us -> 79 us (0.87)
  the two profiles are of different devices: /device:TPU:27 before, /device:TPU:1 now
where the time goes in v3:
time: 79 us; the launch traced here: 78.9 us
  Pallas kernels  75.8 us (96%)
  local copies, waits for them, and re-layouts  1.77 us (2%)
  between operations  1.3 us (2%)
    pallas_call x1, Pallas kernels, body(): pl.pallas_call(kernel, out_shape=jax.ShapeDtypeStruct((1, TILE, inner), j...  75.8 us
    unnamed x1, local copies, waits for them, and re-layouts  1.77 us

profile of v3, /device:TPU:1, one launch (start us, length us, event | category | flops | bytes accessed | tf_op | source)
XLA Modules:
  0.0 78.9 jit_solution(10475346004575137570)
XLA Ops:
  1.3 75.8 %shard_map.82 = bf16[1,128,1536]{2,1,0:T(8,128)(2,1)} custom-call(s32[1,8]{1,0:T(1,128)} %tiles_ref.1, s32[1]{0:T(128)S(6)} %copy.11.count_ref, f32[1]{0:T(128)S(6)} %copy.10.guide_ref, bf16[2,1,128,3072]{3,2,1,0:T(8,128)(2,1)} %hidden_ref.1, bf16[2,1,128,1536]{3,2,1,0:T(8,128)(2,1)} %key_ref.1, bf16[2,1,128,1536]{3,2,1,0:T(8,128)(2,1)} %value_ref.1, ...), custom_call_target="tpu_custom_call" | custom-call | tf_op jit(solution)/shard_map/pallas_call | solution.py:469
  77.1 1.8 %copy.12 = bf16[1,128,1536]{2,1,0:T(8,128)(2,1)} copy(bf16[1,128,1536]{2,1,0:T(8,128)(2,1)} %shard_map.82) | data formatting | bytes 786432

commit v4 on v3

--- a/solution.py
+++ b/solution.py
@@ -13,6 +13,7 @@
 SIDE = 4
 STAGES = 4
 PARTS = 6
+DEPTH = 2
 MESH = pl.DeviceIdType.MESH
 LOG2E = 1.4426950408889634
 
@@ -76,9 +77,11 @@
     row = chip >> 2
     col = chip & (SIDE - 1)
     my_head, has_head = head_of(row, col)
-    odd = col & 1
+    odd = (row + col) & 1
     right = (row * SIDE + ((col + 1) & (SIDE - 1))) * 2 + core
     left = (row * SIDE + ((col - 1) & (SIDE - 1))) * 2 + core
+    below = (((row + 1) & (SIDE - 1)) * SIDE + col) * 2 + core
+    above = (((row - 1) & (SIDE - 1)) * SIDE + col) * 2 + core
     token_count = 2 * SIDE * SIDE
     heads = key_ref.shape[3] // HD
     half_heads = heads // 2
@@ -141,16 +144,21 @@
     def direct_late(k):
         return w_direct(2, 1, 0, k), w_direct(3, 2, 1, k)
 
+    def near_pair(k):
+        return (right, left) if k % 2 == 0 else (below, above)
+
     def pass_early(k):
-        to_1 = jnp.where(odd == 1, token, right)
-        to_2 = jnp.where(odd == 1, token, left)
+        near_1, near_2 = near_pair(k)
+        to_1 = jnp.where(odd == 1, token, near_1)
+        to_2 = jnp.where(odd == 1, token, near_2)
         return (
             w_pass(4, 1, early_1, k, 1 + 2 * odd, jnp.where(odd == 1, up, image), to_1),
             w_pass(5, 2, early_2, k, 2 + odd, jnp.where(odd == 1, down, image), to_2),
         )
 
     def pass_late(k):
-        return w_pass(2, 3, 0, k, 3, image, right), w_pass(3, 3, 1, k, 3, image, left)
+        near_1, near_2 = near_pair(k)
+        return w_pass(2, 3, 0, k, 3, image, near_1), w_pass(3, 3, 1, k, 3, image, near_2)
 
     for k in range(PARTS):
         for copy in direct_early(k):
@@ -277,17 +285,32 @@
         pltpu.make_async_remote_copy(
             src_ref=qsend.at[stage, branch, head - core * half_heads],
             dst_ref=qbuf.at[stage, pl.ds(chip * 2, 2)],
-            send_sem=q_send,
+            send_sem=q_send.at[stage],
             recv_sem=q_recv.at[stage],
             device_id=(image, target),
             device_id_type=MESH,
         ).start()
 
+    def sent(ref, sem):
+        pltpu.make_async_copy(ref, ref, sem).wait()
+
     owns_head = has_head & (row >> 1 == core)
+
+    def q_sent(stage):
+        @pl.when(owns_head)
+        def _():
+            sent(qbuf.at[stage, pl.ds(0, 4 * half_heads - 2)], q_send.at[stage])
+
+        @pl.when(jnp.logical_not(owns_head))
+        def _():
+            sent(qbuf.at[stage, pl.ds(0, 4 * half_heads)], q_send.at[stage])
+
     for stage in range(STAGES):
         for head in range(half_heads):
             block = acc[:, :, stage * rows : (stage + 1) * rows, head * HD : (head + 1) * HD]
             qsend[stage, :, head] = block.astype(jnp.bfloat16)
+        if stage >= DEPTH:
+            q_sent(stage - DEPTH)
 
         for step in range(2 * SIDE):
             to_row = 2 * core + ((row + step) & 1)
@@ -424,9 +447,6 @@
             for copy in pass_late(k):
                 copy.wait_send()
 
-    def sent(ref, sem):
-        pltpu.make_async_copy(ref, ref, sem).wait()
-
     @pl.when(has_head)
     def _():
         sent(kbuf.at[pl.ds(0, 2 * heads - 1)], kv_send.at[0])
@@ -440,13 +460,8 @@
         sent(kbuf.at[pl.ds(0, 2 * heads)], kv_send.at[0])
         sent(vbuf.at[pl.ds(0, 2 * heads)], kv_send.at[1])
 
-    @pl.when(owns_head)
-    def _():
-        sent(qbuf.at[:, pl.ds(0, 4 * half_heads - 2)], q_send)
-
-    @pl.when(jnp.logical_not(owns_head))
-    def _():
-        sent(qbuf.at[:, pl.ds(0, 4 * half_heads)], q_send)
+    for stage in range(STAGES - DEPTH, STAGES):
+        q_sent(stage)
 
     pasted = jnp.int32(0)
     for j in range(slots):
@@ -468,7 +483,7 @@
     dma = pltpu.SemaphoreType.DMA
     return pl.pallas_call(
         kernel,
-        out_shape=jax.ShapeDtypeStruct((1, TILE, inner), jnp.bfloat16),
+        out_shape=pltpu.VMEM((1, TILE, inner), jnp.bfloat16),
         in_specs=[pl.BlockSpec(memory_space=pltpu.SMEM)] * 3
         + [pl.BlockSpec(memory_space=pl.ANY)] * 5,
         out_specs=pl.BlockSpec(memory_space=pltpu.VMEM),
@@ -495,7 +510,7 @@
             dma((images - 1, 2, PARTS)),
             dma((2,)),
             dma((2,)),
-            dma,
+            dma((STAGES,)),
             dma((STAGES,)),
             dma((STAGES,)),
             dma((STAGES,)),

time: 79 us -> 71.7 us (0.908)
  Pallas kernels: 75.8 us -> 69.5 us
  local copies, waits for them, and re-layouts: 1.77 us -> 0.75 us
    pallas_call x1, Pallas kernels: 75.8 us -> 69.5 us  [body(): pl.pallas_call(kernel, out_shape=pltpu.VMEM((1, TILE, inner), jnp.bfloat1...]
    unnamed x1, local copies, waits for them, and re-layouts: 1.77 us -> 0.75 us
where the time goes in v4:
time: 71.7 us; the launch traced here: 71.6 us
  Pallas kernels  69.5 us (97%)
  between operations  1.3 us (2%)
  local copies, waits for them, and re-layouts  0.75 us (1%)
    pallas_call x1, Pallas kernels, body(): pl.pallas_call(kernel, out_shape=pltpu.VMEM((1, TILE, inner), jnp.bfloat1...  69.5 us

profile of v4, /device:TPU:1, one launch (start us, length us, event | category | flops | bytes accessed | tf_op | source)
XLA Modules:
  0.0 71.6 jit_solution(1160497502902128490)
XLA Ops:
  1.3 69.5 %shard_map.82 = bf16[1,128,1536]{2,1,0:T(8,128)(2,1)S(1)} custom-call(s32[1,8]{1,0:T(1,128)} %tiles_ref.1, s32[1]{0:T(128)S(6)} %copy.12.count_ref, f32[1]{0:T(128)S(6)} %copy.11.guide_ref, bf16[2,1,128,3072]{3,2,1,0:T(8,128)(2,1)} %hidden_ref.1, bf16[2,1,128,1536]{3,2,1,0:T(8,128)(2,1)} %key_ref.1, bf16[2,1,128,1536]{3,2,1,0:T(8,128)(2,1)} %value_ref.1, ...), custom_call_target="tpu_custom_call" | custom-call | tf_op jit(solution)/shard_map/pallas_call | solution.py:484
  70.8 0.7 %copy.10 = bf16[1,128,1536]{2,1,0:T(8,128)(2,1)} copy(bf16[1,128,1536]{2,1,0:T(8,128)(2,1)S(1)} %shard_map.82) | data formatting | bytes 786432

commit v5 on v4

--- a/solution.py
+++ b/solution.py
@@ -12,7 +12,7 @@
 TILE = 128
 SIDE = 4
 STAGES = 4
-PARTS = 6
+PARTS = 12
 DEPTH = 2
 MESH = pl.DeviceIdType.MESH
 LOG2E = 1.4426950408889634
@@ -109,66 +109,46 @@
         pl.semaphore_signal(barrier, inc=1, device_id=(image, peer), device_id_type=MESH)
     pl.semaphore_wait(barrier, token_count - 1 + 2)
 
-    half = depth // 2
-    piece = half // PARTS
-    early_1, early_2 = 1 - odd, odd
-
-    def w_rows(part, k):
-        return pl.ds(pl.multiple_of(part * half + k * piece, piece), piece)
-
-    def w_copy(index, src, slot, part, k, to_image, to_token):
+    piece = depth // PARTS
+    third = depth // 3
+    even = odd == 0
+    base = 4 * (1 - odd)
+
+    def w_index(side, k):
+        return k if side == 0 else PARTS - 1 - k
+
+    def w_rows(side, k):
+        return pl.ds(pl.multiple_of(w_index(side, k) * piece, piece), piece)
+
+    def w_copy(kind, src, slot, side, k, to_image, to_token):
         return pltpu.make_async_remote_copy(
             src_ref=src,
-            dst_ref=wbuf.at[slot, w_rows(part, k)],
-            send_sem=w_send.at[index, k],
-            recv_sem=w_recv.at[slot - 1, part, k],
+            dst_ref=wbuf.at[slot, w_rows(side, k)],
+            send_sem=w_send.at[kind],
+            recv_sem=w_recv.at[slot - 1, w_index(side, k)],
             device_id=(to_image, to_token),
             device_id_type=MESH,
         )
 
-    def w_direct(index, slot, part, k):
-        near = up if slot == 1 else down
-        return w_copy(index, w_ref.at[w_rows(part, k), my_cols], slot, part, k, near, token)
-
-    def w_pass(index, slot, part, k, new_slot, to_image, to_token):
-        src = wbuf.at[slot, w_rows(part, k)]
-        return w_copy(index, src, new_slot, part, k, to_image, to_token)
-
-    def w_wait(slot, part, k):
-        dst = wbuf.at[slot, w_rows(part, k)]
-        pltpu.make_async_copy(dst, dst, w_recv.at[slot - 1, part, k]).wait()
-
-    def direct_early(k):
-        return w_direct(0, 1, early_1, k), w_direct(1, 2, early_2, k)
-
-    def direct_late(k):
-        return w_direct(2, 1, 0, k), w_direct(3, 2, 1, k)
-
-    def near_pair(k):
-        return (right, left) if k % 2 == 0 else (below, above)
-
-    def pass_early(k):
-        near_1, near_2 = near_pair(k)
-        to_1 = jnp.where(odd == 1, token, near_1)
-        to_2 = jnp.where(odd == 1, token, near_2)
-        return (
-            w_pass(4, 1, early_1, k, 1 + 2 * odd, jnp.where(odd == 1, up, image), to_1),
-            w_pass(5, 2, early_2, k, 2 + odd, jnp.where(odd == 1, down, image), to_2),
-        )
-
-    def pass_late(k):
-        near_1, near_2 = near_pair(k)
-        return w_pass(2, 3, 0, k, 3, image, near_1), w_pass(3, 3, 1, k, 3, image, near_2)
-
-    for k in range(PARTS):
-        for copy in direct_early(k):
-            copy.start()
-
-    @pl.when(odd == 0)
-    def _():
-        for k in range(PARTS):
-            for copy in direct_late(k):
-                copy.start()
+    def w_direct(side, k):
+        near = up if side == 0 else down
+        w_copy(0, w_ref.at[w_rows(side, k), my_cols], 1 + side, side, k, near, token).start()
+
+    def w_relay(side, k):
+        near = up if side == 0 else down
+        w_copy(0, wbuf.at[1 + side, w_rows(side, k)], 3, side, k, near, token).start()
+
+    def w_pass(slot, side, k, turn):
+        near = ((right, below), (left, above))[side][turn % 2]
+        w_copy(1, wbuf.at[slot, w_rows(side, k)], slot, side, k, image, near).start()
+
+    def w_wait(slot, side, k):
+        dst = wbuf.at[slot, w_rows(side, k)]
+        pltpu.make_async_copy(dst, dst, w_recv.at[slot - 1, w_index(side, k)]).wait()
+
+    for k in range(4):
+        for side in range(2):
+            w_direct(side, base + k)
 
     hid_out = pltpu.make_async_remote_copy(
         src_ref=hidden_ref.at[:, 0],
@@ -225,7 +205,8 @@
     rows_all = 4 * TILE
     width = 256
 
-    def project(slot, owner, start, size, is_first):
+    def project(slot, start, size, is_first=False):
+        owner = jnp.where(slot == 0, image, jnp.where(slot == 1, down, jnp.where(slot == 2, up, far)))
         features = pl.ds(pl.multiple_of(owner * depth + start, 128), size)
         w_part = pl.ds(pl.multiple_of(start, 128), size)
 
@@ -245,39 +226,73 @@
     w_own.wait()
     hid_own.wait()
     hid_out.wait_recv()
-    project(0, image, 0, depth, True)
-    for k in range(PARTS):
-        first, second = pass_early(k)
-        w_wait(1, early_1, k)
-        first.start()
-        w_wait(2, early_2, k)
-        second.start()
-    project(1, down, early_1 * half, half, False)
-    project(2, up, early_2 * half, half, False)
+    project(0, 0, depth, True)
+    for k in range(4):
+        for side in range(2):
+            w_wait(1 + side, side, base + k)
+            if k < 2:
+                w_relay(side, base + k)
+            w_pass(1 + side, side, base + k, k)
+
+        if k == 1:
+
+            @pl.when(even)
+            def _():
+                for late in range(4):
+                    for side in range(2):
+                        w_direct(side, 8 + late)
+
+        if k >= 2:
+
+            @pl.when(odd == 1)
+            def _():
+                for side in range(2):
+                    w_relay(side, k)
+
+    near_0, near_1 = (1 - odd) * third, (1 + odd) * third
+    project(1, near_0, third)
+    project(2, near_1, third)
+
+    @pl.when(even)
+    def _():
+        for k in range(4, 6):
+            for side in range(2):
+                w_wait(3, side, k)
+                w_pass(3, side, k, k)
+        for k in range(8, 12):
+            for side in range(2):
+                w_wait(1 + side, side, k)
+                w_pass(1 + side, side, k, k)
 
     @pl.when(odd == 1)
     def _():
-        for k in range(PARTS):
-            first, second = pass_late(k)
-            w_wait(3, 0, k)
-            first.start()
-            w_wait(3, 1, k)
-            second.start()
-
-    for k in range(PARTS):
-        w_wait(1, 1 - early_1, k)
-    project(1, down, (1 - early_1) * half, half, False)
-    for k in range(PARTS):
-        w_wait(2, 1 - early_2, k)
-    project(2, up, (1 - early_2) * half, half, False)
-
-    @pl.when(odd == 0)
-    def _():
-        for k in range(PARTS):
-            w_wait(3, 0, k)
-            w_wait(3, 1, k)
-
-    project(3, far, 0, depth, False)
+        for k in range(4):
+            for side in range(2):
+                w_wait(3, side, k)
+                w_pass(3, side, k, k)
+
+    project(1 + 2 * odd, 2 * third * (1 - odd), third)
+    project(2 + odd, 2 * third * odd, third)
+
+    for side in range(2):
+        for k in range(4):
+            w_wait(1 + side, side, 4 * odd + k)
+    project(1, odd * third, third)
+    project(2, (2 - odd) * third, third)
+
+    @pl.when(odd == 1)
+    def _():
+        for side in range(2):
+            for k in range(4, 6):
+                w_wait(3, side, k)
+
+    project(3, third, third)
+    last_0, last_1 = 3 - 2 * odd, 3 - odd
+    for side in range(2):
+        for k in range(4):
+            w_wait((last_0, last_1)[side], side, 8 * odd + k)
+    project(last_0, 2 * third * odd, third)
+    project(last_1, 2 * third * (1 - odd), third)
 
     rows = TILE // STAGES
 
@@ -431,21 +446,16 @@
                 deliver(stage - 1)
 
     hid_out.wait_send()
-    for k in range(PARTS):
-        for copy in direct_early(k) + pass_early(k):
-            copy.wait_send()
-
-    @pl.when(odd == 0)
-    def _():
-        for k in range(PARTS):
-            for copy in direct_late(k):
-                copy.wait_send()
+
+    @pl.when(even)
+    def _():
+        for kind in range(2):
+            sent(wbuf.at[pl.ds(0, 2), pl.ds(0, 10 * piece)], w_send.at[kind])
 
     @pl.when(odd == 1)
     def _():
-        for k in range(PARTS):
-            for copy in pass_late(k):
-                copy.wait_send()
+        for kind in range(2):
+            sent(wbuf.at[pl.ds(0, 2), pl.ds(0, 8 * piece)], w_send.at[kind])
 
     @pl.when(has_head)
     def _():
@@ -506,8 +516,8 @@
             pltpu.SMEM((tokens,), jnp.int32),
             dma((3,)),
             dma((2,)),
-            dma((6, PARTS)),
-            dma((images - 1, 2, PARTS)),
+            dma((2,)),
+            dma((images - 1, PARTS)),
             dma((2,)),
             dma((2,)),
             dma((STAGES,)),

time: 71.7 us -> 74.7 us (1.042)
  Pallas kernels: 69.5 us -> 72.1 us
    pallas_call x1, Pallas kernels: 69.5 us -> 72.1 us  [body(): pl.pallas_call(kernel, out_shape=pltpu.VMEM((1, TILE, inner), jnp.bfloat1...]
where the time goes in v5:
time: 74.7 us; the launch traced here: 74.2 us
  Pallas kernels  72.1 us (97%)
  between operations  1.3 us (2%)
  local copies, waits for them, and re-layouts  0.75 us (1%)
    pallas_call x1, Pallas kernels, body(): pl.pallas_call(kernel, out_shape=pltpu.VMEM((1, TILE, inner), jnp.bfloat1...  72.1 us

profile of v5, /device:TPU:1, one launch (start us, length us, event | category | flops | bytes accessed | tf_op | source)
XLA Modules:
  0.0 74.2 jit_solution(2196534589352343448)
XLA Ops:
  1.3 72.1 %shard_map.82 = bf16[1,128,1536]{2,1,0:T(8,128)(2,1)S(1)} custom-call(s32[1,8]{1,0:T(1,128)} %tiles_ref.1, s32[1]{0:T(128)S(6)} %copy.12.count_ref, f32[1]{0:T(128)S(6)} %copy.11.guide_ref, bf16[2,1,128,3072]{3,2,1,0:T(8,128)(2,1)} %hidden_ref.1, bf16[2,1,128,1536]{3,2,1,0:T(8,128)(2,1)} %key_ref.1, bf16[2,1,128,1536]{3,2,1,0:T(8,128)(2,1)} %value_ref.1, ...), custom_call_target="tpu_custom_call" | custom-call | tf_op jit(solution)/shard_map/pallas_call | solution.py:494
  73.4 0.7 %copy.10 = bf16[1,128,1536]{2,1,0:T(8,128)(2,1)} copy(bf16[1,128,1536]{2,1,0:T(8,128)(2,1)S(1)} %shard_map.82) | data formatting | bytes 786432

commit v6 on v4

--- a/solution.py
+++ b/solution.py
@@ -14,6 +14,8 @@
 STAGES = 4
 PARTS = 6
 DEPTH = 2
+BLOCK = 32
+SPAN = 8
 MESH = pl.DeviceIdType.MESH
 LOG2E = 1.4426950408889634
 
@@ -47,7 +49,11 @@
     qnow,
     kbuf,
     vbuf,
+    query,
     score,
+    heavy,
+    totals,
+    sums,
     attended,
     other,
     guided,
@@ -336,7 +342,7 @@
     mine_rows = pl.ds(pl.multiple_of(core * share, share), share)
     sent_rows = pl.ds(pl.multiple_of((1 - core) * share, share), share)
     factor = LOG2E / math.sqrt(HD)
-    span = 8
+    span = SPAN
     chunk = span * TILE
     chunks = token_count // span
     height = slots * rows
@@ -369,29 +375,51 @@
 
     def attention(stage):
         qnow[...] = qbuf[stage]
-        query = jnp.concatenate([qnow[tiles_ref[0, j]] for j in range(slots)], axis=0)
-        peak = jnp.full((height, 128), -jnp.inf, jnp.float32)
+        for j in range(slots):
+            query[j * rows : (j + 1) * rows] = qnow[tiles_ref[0, j]]
+
+        def logits(part):
+            keys = kbuf[part * span : (part + 1) * span].reshape(chunk, HD)
+            score[part % 2] = lax.dot_general(
+                query[...], keys, (((1,), (1,)), ((), ())), preferred_element_type=jnp.float32
+            )
+
+        blocks = range(0, height, BLOCK)
+        top = [None for _ in blocks]
+        logits(0)
         for part in range(chunks):
-            keys = kbuf[part * span : (part + 1) * span].reshape(chunk, HD)
-            logits = lax.dot_general(
-                query, keys, (((1,), (1,)), ((), ())), preferred_element_type=jnp.float32
-            )
-            score[:, part * chunk : (part + 1) * chunk] = logits
-            for lane in range(span):
-                peak = jnp.maximum(peak, logits[:, lane * 128 : (lane + 1) * 128])
-        top = jnp.max(peak, axis=-1, keepdims=True) * factor
-        total = jnp.zeros((height, 128), jnp.float32)
-        summed = jnp.zeros((height, HD), jnp.float32)
-        for part in range(chunks):
+            if part + 1 < chunks:
+                logits(part + 1)
+            shrink = []
+            for index, low in enumerate(blocks):
+                some = pl.ds(low, BLOCK)
+                peak = score[part % 2, some, 0:128]
+                for lane in range(1, span):
+                    peak = jnp.maximum(peak, score[part % 2, some, lane * 128 : (lane + 1) * 128])
+                peak = jnp.max(peak, axis=-1, keepdims=True) * factor
+                if part > 0:
+                    peak = jnp.maximum(peak, top[index])
+                    shrink.append(jnp.exp2(top[index] - peak))
+                top[index] = peak
+                total = None
+                for lane in range(span):
+                    lanes = slice(lane * 128, (lane + 1) * 128)
+                    weight = jnp.exp2(score[part % 2, some, lanes] * factor - peak)
+                    heavy[part % 2, some, lanes] = weight.astype(jnp.bfloat16)
+                    total = weight if total is None else total + weight
+                if part > 0:
+                    total = total + totals[some] * shrink[index]
+                totals[some] = total
             values = vbuf[part * span : (part + 1) * span].reshape(chunk, HD)
-            weight = jnp.exp2(score[:, part * chunk : (part + 1) * chunk] * factor - top)
-            for lane in range(span):
-                total = total + weight[:, lane * 128 : (lane + 1) * 128]
-            summed = summed + jnp.dot(
-                weight.astype(jnp.bfloat16), values, preferred_element_type=jnp.float32
-            )
-        summed = summed / jnp.sum(total, axis=-1, keepdims=True)
-        attended[stage] = summed.reshape(slots, rows, HD)
+            summed = jnp.dot(heavy[part % 2], values, preferred_element_type=jnp.float32)
+            for index, low in enumerate(blocks):
+                some = pl.ds(low, BLOCK)
+                block = summed[low : low + BLOCK]
+                if part > 0:
+                    block = block + sums[some] * shrink[index]
+                sums[some] = block
+        done = sums[...] / jnp.sum(totals[...], axis=-1, keepdims=True)
+        attended[stage] = done.reshape(slots, rows, HD)
 
     def deliver(stage):
         exchange(stage).wait_recv()
@@ -496,7 +524,11 @@
             pltpu.VMEM((tokens, rows, HD), jnp.bfloat16),
             pltpu.VMEM((tokens, TILE, HD), jnp.bfloat16),
             pltpu.VMEM((tokens, TILE, HD), jnp.bfloat16),
-            pltpu.VMEM((slots * rows, tokens * TILE), jnp.float32),
+            pltpu.VMEM((slots * rows, HD), jnp.bfloat16),
+            pltpu.VMEM((2, slots * rows, SPAN * TILE), jnp.float32),
+            pltpu.VMEM((2, slots * rows, SPAN * TILE), jnp.bfloat16),
+            pltpu.VMEM((slots * rows, 128), jnp.float32),
+            pltpu.VMEM((slots * rows, HD), jnp.float32),
             pltpu.VMEM((STAGES, slots, rows, HD), jnp.float32),
             pltpu.VMEM((STAGES, slots, rows // 2, HD), jnp.float32),
             pltpu.VMEM((STAGES, slots, rows // 2, HD), jnp.bfloat16),

time: 71.7 us -> 70.7 us (0.986)
  Pallas kernels: 69.5 us -> 68.6 us
    pallas_call x1, Pallas kernels: 69.5 us -> 68.6 us  [body(): pl.pallas_call(kernel, out_shape=pltpu.VMEM((1, TILE, inner), jnp.bfloat1...]
where the time goes in v6:
time: 70.7 us; the launch traced here: 70.6 us
  Pallas kernels  68.6 us (97%)
  between operations  1.3 us (2%)
  local copies, waits for them, and re-layouts  0.75 us (1%)
    pallas_call x1, Pallas kernels, body(): pl.pallas_call(kernel, out_shape=pltpu.VMEM((1, TILE, inner), jnp.bfloat1...  68.6 us

profile of v6, /device:TPU:1, one launch (start us, length us, event | category | flops | bytes accessed | tf_op | source)
XLA Modules:
  0.0 70.6 jit_solution(10754746481743447113)
XLA Ops:
  1.3 68.6 %shard_map.82 = bf16[1,128,1536]{2,1,0:T(8,128)(2,1)S(1)} custom-call(s32[1,8]{1,0:T(1,128)} %tiles_ref.1, s32[1]{0:T(128)S(6)} %copy.12.count_ref, f32[1]{0:T(128)S(6)} %copy.11.guide_ref, bf16[2,1,128,3072]{3,2,1,0:T(8,128)(2,1)} %hidden_ref.1, bf16[2,1,128,1536]{3,2,1,0:T(8,128)(2,1)} %key_ref.1, bf16[2,1,128,1536]{3,2,1,0:T(8,128)(2,1)} %value_ref.1, ...), custom_call_target="tpu_custom_call" | custom-call | tf_op jit(solution)/shard_map/pallas_call | solution.py:512
  69.9 0.7 %copy.10 = bf16[1,128,1536]{2,1,0:T(8,128)(2,1)} copy(bf16[1,128,1536]{2,1,0:T(8,128)(2,1)S(1)} %shard_map.82) | data formatting | bytes 786432

commit v7 on v6

--- a/solution.py
+++ b/solution.py
@@ -170,12 +170,6 @@
         for copy in direct_early(k):
             copy.start()
 
-    @pl.when(odd == 0)
-    def _():
-        for k in range(PARTS):
-            for copy in direct_late(k):
-                copy.start()
-
     hid_out = pltpu.make_async_remote_copy(
         src_ref=hidden_ref.at[:, 0],
         dst_ref=hid.at[:, core],
@@ -219,6 +213,12 @@
         kv_start(my_head, 1 - core, partner)
         for src, dst, kind in kv_pairs(my_head, core):
             pltpu.make_async_copy(src, dst, kv_recv.at[kind]).start()
+
+    @pl.when(odd == 0)
+    def _():
+        for k in range(PARTS):
+            for copy in direct_late(k):
+                copy.start()
 
     @pl.loop(0, token_count)
     def _(tile):

time: 70.7 us -> 70 us (0.990)
  Pallas kernels: 68.6 us -> 67.7 us
    pallas_call x1, Pallas kernels: 68.6 us -> 67.7 us  [body(): pl.pallas_call(kernel, out_shape=pltpu.VMEM((1, TILE, inner), jnp.bfloat1...]
where the time goes in v7:
time: 70 us; the launch traced here: 69.8 us
  Pallas kernels  67.7 us (97%)
  between operations  1.3 us (2%)
  local copies, waits for them, and re-layouts  0.75 us (1%)
    pallas_call x1, Pallas kernels, body(): pl.pallas_call(kernel, out_shape=pltpu.VMEM((1, TILE, inner), jnp.bfloat1...  67.7 us

profile of v7, /device:TPU:1, one launch (start us, length us, event | category | flops | bytes accessed | tf_op | source)
XLA Modules:
  0.0 69.8 jit_solution(10455928358360571815)
XLA Ops:
  1.3 67.7 %shard_map.82 = bf16[1,128,1536]{2,1,0:T(8,128)(2,1)S(1)} custom-call(s32[1,8]{1,0:T(1,128)} %tiles_ref.1, s32[1]{0:T(128)S(6)} %copy.12.count_ref, f32[1]{0:T(128)S(6)} %copy.11.guide_ref, bf16[2,1,128,3072]{3,2,1,0:T(8,128)(2,1)} %hidden_ref.1, bf16[2,1,128,1536]{3,2,1,0:T(8,128)(2,1)} %key_ref.1, bf16[2,1,128,1536]{3,2,1,0:T(8,128)(2,1)} %value_ref.1, ...), custom_call_target="tpu_custom_call" | custom-call | tf_op jit(solution)/shard_map/pallas_call | solution.py:512
  69.0 0.7 %copy.10 = bf16[1,128,1536]{2,1,0:T(8,128)(2,1)} copy(bf16[1,128,1536]{2,1,0:T(8,128)(2,1)S(1)} %shard_map.82) | data formatting | bytes 786432
